TPU v7x, 512 devices: a whole 4x4x16 slice. The times are simulated.
512 devices in a mesh: dp: 32 (over x, y, core), seq: 16 (over z).
Axes of the slice: x: 4, y: 4, z: 16, core: 2. Of those that a mesh axis runs over, the one named last changes fastest.
Arguments:
- tiles: bfloat16 [16384, 2, 8, 8, 192], P(('dp', 'seq')), may hold values from -6 to 6
- tile_dest: int32 [16384], P(('dp', 'seq')), may hold values from 0 to 31, as said below
- tile_meta: int32 [16384, 4], P(('dp', 'seq')), may hold values from 0 to 63, as said below
- space_weight: bfloat16 [1728, 192], replicated, may hold values from -0.15625 to 0.15625
- time_weight: bfloat16 [576, 192], replicated, may hold values from -0.25 to 0.25
- conv_bias: float32 [192], replicated, may hold values from -3 to 3
- latent_weight: bfloat16 [192, 16], replicated, may hold values from -0.4375 to 0.4375
- embed_weight: bfloat16 [64, 5120], replicated, may hold values from -0.75 to 0.75
- qkv_weight: bfloat16 [5120, 384], P('seq'), may hold values from -2 to 2
- rope_freq: float32 [64], replicated, may hold values from 0.05 to 1
- cotangent: bfloat16 [131072, 128], P(('dp', 'seq')), may hold values from -16 to 16
Outputs:
- attended: bfloat16 [131072, 128], P(('dp', 'seq'))
- freq_grad: float32 [64], replicated
Inputs may be any that keep to these rules, and one draw needn't show every extreme that they name: `tile_dest`: among the tiles of one device, at most 2 name one dp index. Every owner receives at most 64 tiles; in every draw, in every seq index, some owner receives exactly 64, 2 from every loader. `tile_meta`: column 0 numbers the tiles of one owner 0, 1, 2 and so on without gaps; columns 1 to 3 are not negative and below 64.
All inputs are finite; a program needn't handle non-finite values.
Results may differ from a plain program's by a relative error of at most 0.034.
Values may be sent and summed in bfloat16 or wider, within the bound.
A program may use at most 128 MiB of HBM per device.

v0:
```python
import functools
import math

import jax
import jax.numpy as jnp
from jax import lax
from jax.experimental import pallas as pl
from jax.experimental.pallas import tpu as pltpu
from jax.sharding import PartitionSpec as P

F32 = jnp.float32
BF16 = jnp.bfloat16
META = 128
BIG = 1e30


def iota(shape, dim):
    return lax.broadcasted_iota(jnp.int32, shape, dim)


def dot(a, b):
    return jnp.dot(a, b, preferred_element_type=F32)


def dot_nt(a, b):
    return lax.dot_general(a, b, (((1,), (1,)), ((), ())), preferred_element_type=F32)


def encode_tiles(tiles_ref, space_ref, time_ref, bias_ref, latent_ref):
    held, frames, height, width, chans = tiles_ref.shape
    out_h = height // 2
    rows = held * width
    lat_wide = latent_ref.shape[1]
    total = jnp.zeros((rows, lat_wide), F32)
    lane = iota((rows, lat_wide), 1)
    col = iota((rows, lat_wide), 0) % width
    lane_h = 2 * (lane // 128) + (lane // 32) % 2
    lane_w = 2 * ((lane // 64) % 2) + (lane // 16) % 2
    at_col = 2 * lane_w == col
    edge = iota((1, width, chans), 1) < width - 2
    for h in range(out_h):
        shifted = [None, None, None]
        for row_off in range(3):
            src = 2 * h + row_off
            if src >= height:
                continue
            x = tiles_ref[:, :, src].reshape(held * frames * width, chans)
            for col_off in range(3):
                tap = (row_off * 3 + col_off) * chans
                part = dot(x, space_ref[tap : tap + chans, :])
                old = shifted[col_off]
                shifted[col_off] = part if old is None else old + part
        y0, y1, y2 = [y.reshape(held * frames, width, chans) for y in shifted]
        y1 = pltpu.roll(y1, width - 1, axis=1)
        y2 = jnp.where(edge, pltpu.roll(y2, width - 2, axis=1), 0.0)
        spatial = (y0 + y1 + y2).reshape(held, frames, width, chans)
        first = spatial[:, 0].reshape(rows, chans).astype(BF16)
        second = spatial[:, 1].reshape(rows, chans).astype(BF16)
        summed = dot(first, time_ref[chans : 2 * chans, :]) + dot(second, time_ref[2 * chans :, :])
        summed = summed + bias_ref[...]
        feats = (summed / (1.0 + jnp.exp(-summed))).astype(BF16)
        latents = dot(feats, latent_ref[...])
        total = total + jnp.where((lane_h == h) & at_col, latents, 0.0)
    return total.astype(BF16)


def encode_kernel(tiles_ref, space_ref, time_ref, bias_ref, latent_ref, slot8_ref, slot_ref, meta_ref, out_ref):
    latents = encode_tiles(tiles_ref, space_ref, time_ref, bias_ref, latent_ref)
    slots = out_ref.shape[0]
    rows = latents.shape[0]
    held = meta_ref.shape[0]
    pick = (iota((slots, rows), 0) == slot8_ref[...]).astype(F32).astype(BF16)
    out_ref[:, 0:256] = dot(pick, latents).astype(BF16)
    pick = (iota((slots, held), 0) == slot_ref[...]).astype(F32).astype(BF16)
    out_ref[:, 256:] = dot(pick, meta_ref[...]).astype(BF16)


def sincos(angle):
    turns = jnp.floor(angle * (0.5 / math.pi) + 0.5)
    r = angle - turns * 6.28125
    r = r - turns * (2.0 * math.pi - 6.28125)
    z = r * r
    s = jnp.full_like(z, -1.0 / math.factorial(15))
    for n in (13, 11, 9, 7, 5, 3, 1):
        s = s * z + (1.0 if n % 4 == 1 else -1.0) / math.factorial(n)
    c = jnp.full_like(z, 1.0 / math.factorial(16))
    for n in (14, 12, 10, 8, 6, 4, 2, 0):
        c = c * z + (1.0 if n % 4 == 0 else -1.0) / math.factorial(n)
    return s * r, c


def axis_masks(shape):
    pair = iota(shape, 1) % 64
    return pair < 22, (pair >= 22) & (pair < 43), pair >= 43


def swap_halves(u):
    lane = iota(u.shape, 1)
    turned = pltpu.roll(u, 64, axis=1)
    return jnp.where(lane < 64, -turned, turned)


def rotary_tables(freq):
    shape = (META, META)
    sub = iota(shape, 0)
    in_f, in_r, in_c = axis_masks(shape)
    step = jnp.where((sub == 1) & in_f, 1.0, 0.0)
    step = jnp.where(((sub == 2) & in_r) | ((sub == 3) & in_c), 2.0, step)
    rest = freq
    tables = []
    for _ in range(3):
        part = rest.astype(BF16).astype(F32)
        rest = rest - part
        tables.append((step * part).astype(BF16))
    return tables, step.astype(BF16)


def token_weights(ew_ref, freq, first):
    base = ew_ref[:, first : first + 128]
    shape = (8, 128)
    in_f, in_r, in_c = axis_masks(shape)
    blocks = []
    for tok in range(4):
        row_block, col_block = tok // 2, tok % 2
        offset = jnp.where(in_r, float(row_block), 0.0) + jnp.where(in_c, float(col_block), 0.0)
        s, c = sincos(jnp.broadcast_to(freq, shape) * offset)
        turned = base * c[0:1, :] + swap_halves(base) * s[0:1, :]
        blocks.append(jnp.concatenate([turned, swap_halves(turned)], axis=1))
    return jnp.concatenate(blocks, axis=0)


def attend_kernel(own_ref, all_ref, ew_ref, freq_ref, cot_ref, out_ref, grad_ref, keys_ref, vals_ref, score_ref):
    tiles = all_ref.shape[0]
    slots = own_ref.shape[0]
    tokens = 4 * slots
    keys = 4 * tiles
    freq = freq_ref[...]
    scale = 128.0 ** (-0.5)
    tables, step = rotary_tables(freq)

    def positions(meta):
        angle = dot(meta, tables[0]) + dot(meta, tables[1]) + dot(meta, tables[2])
        s, c = sincos(angle)
        return s, c, dot(meta, step)

    wk = token_weights(ew_ref, freq, 128)
    wq = token_weights(ew_ref, freq, 0)
    wv = ew_ref[:, 256:384]
    row4 = iota((256, 128), 0) // 64

    own = own_ref[...]
    pick8 = (iota((8, META), 0) == iota((8, META), 1)).astype(F32).astype(BF16)
    slot_meta = dot_nt(pick8, own[:, 256:])
    place_row = iota((tokens, slots), 0) // 4
    taken = (place_row.astype(F32) == slot_meta[0:1, :]) & (slot_meta[4:5, :] > 0.5)
    mine = dot(jnp.where(taken, 1.0, 0.0).astype(BF16), own)
    which = iota((tokens, 256), 0) % 4 == iota((tokens, 256), 1) // 64
    my_lat = jnp.where(which, mine[:, 0:256], 0.0).astype(BF16)
    my_meta = mine[:, 256:].astype(BF16)
    live = mine[:, 260:261]
    s, c, pos = positions(my_meta)
    u = dot(my_lat, wq.astype(BF16))
    q = u[:, 0:128] * c + u[:, 128:256] * s
    in_f, in_r, in_c = axis_masks((tokens, 128))
    tok = iota((tokens, 128), 0) % 4
    pos = pos + jnp.where(in_r, (tok // 2).astype(F32), 0.0) + jnp.where(in_c, (tok % 2).astype(F32), 0.0)
    lane4 = jnp.where(iota((tokens, META), 1) == 4, 1.0, 0.0).astype(BF16)
    q_ext = jnp.concatenate([lane4, (q * (scale * math.log2(math.e))).astype(BF16)], axis=1)

    block = min(256, tiles)
    for start in range(0, tiles, block):
        lat = all_ref[start : start + block, 0:256]
        meta = all_ref[start : start + block, 256:]
        s, c, kpos = positions(meta)
        dead = jnp.where(iota((block, META), 1) == 4, (meta.astype(F32) - 1.0) * BIG, 0.0).astype(BF16)
        in_f, in_r, in_c = axis_masks((1, 128))
        for tok in range(4):
            here = jnp.where(row4 == tok, jnp.concatenate([wv] * 4, axis=0), 0.0).astype(BF16)
            wide = jnp.where(iota((256, 256), 0) // 64 == tok, wk, 0.0).astype(BF16)
            u = dot(lat, wide)
            k = u[:, 0:128] * c + u[:, 128:256] * s
            offset = jnp.where(in_r, float(tok // 2), 0.0) + jnp.where(in_c, float(tok % 2), 0.0)
            at = tok * tiles + start
            keys_ref[at : at + block, 0:128] = dead
            keys_ref[at : at + block, 128:256] = k.astype(BF16)
            keys_ref[at : at + block, 256:384] = (k * (kpos + offset)).astype(BF16)
            vals_ref[at : at + block, :] = dot(lat, here).astype(BF16)

    chunk = 512
    starts = range(0, keys, chunk)
    top = jnp.full((tokens, chunk), -jnp.inf, F32)
    for at in starts:
        scores = dot_nt(q_ext, keys_ref[at : at + chunk, 0:256])
        score_ref[:, at : at + chunk] = scores
        top = jnp.maximum(top, scores)
    top = jnp.max(top, axis=1, keepdims=True)
    sums = jnp.zeros((tokens, chunk), F32)
    mixed = jnp.zeros((tokens, 128), F32)
    for at in starts:
        weights = jnp.exp2(score_ref[:, at : at + chunk] - top)
        score_ref[:, at : at + chunk] = weights
        sums = sums + weights
        mixed = mixed + dot(weights.astype(BF16), vals_ref[at : at + chunk, :])
    inv = 1.0 / jnp.sum(sums, axis=1, keepdims=True)
    mixed = mixed * inv
    out_ref[...] = (mixed * live).astype(BF16)
    cot = cot_ref[...]
    mean = jnp.sum(cot.astype(F32) * mixed, axis=1, keepdims=True)
    back = jnp.zeros((tokens, 256), F32)
    for at in starts:
        dprob = dot_nt(cot, vals_ref[at : at + chunk, :])
        dscore = score_ref[:, at : at + chunk] * (dprob - mean)
        back = back + dot(dscore.astype(BF16), keys_ref[at : at + chunk, 128:384])
    row_fac = inv * live * scale
    g = pltpu.roll(back[:, 0:128], 64, axis=1)
    gp = pltpu.roll(back[:, 128:256], 64, axis=1)
    terms = q * (pos * g - gp) * row_fac
    line = jnp.sum(terms, axis=0, keepdims=True)
    lane = iota((1, 128), 1)
    other = pltpu.roll(line, 64, axis=1)
    grad_ref[...] = jnp.where(lane < 64, line - other, other - line)


def per_device(
    tiles,
    tile_dest,
    tile_meta,
    space_weight,
    time_weight,
    conv_bias,
    latent_weight,
    embed_weight,
    qkv_weight,
    rope_freq,
    cotangent,
):
    loaders = lax.axis_size("dp")
    held = tiles.shape[0]
    slots = 2 * held
    capacity = slots // loaders
    order = jnp.arange(held, dtype=jnp.int32)
    same = (tile_dest[:, None] == tile_dest[None, :]) & (order[:, None] < order[None, :])
    rank = jnp.sum(same.astype(jnp.int32), axis=0)
    slot = tile_dest * capacity + rank
    meta = jnp.concatenate([tile_meta, jnp.ones((held, 1), jnp.int32)], axis=1)
    meta = jnp.pad(meta, ((0, 0), (0, META - 5))).astype(BF16)
    outgoing = pl.pallas_call(
        encode_kernel,
        out_shape=jax.ShapeDtypeStruct((slots, 256 + META), BF16),
        compiler_params=pltpu.CompilerParams(vmem_limit_bytes=48 << 20),
    )(
        tiles,
        space_weight,
        time_weight,
        conv_bias[None, :],
        jnp.tile(latent_weight, (1, 16)),
        jnp.repeat(slot, tiles.shape[3])[None, :],
        slot[None, :],
        meta,
    )
    shard = qkv_weight.shape[0]
    mine = lax.dynamic_slice_in_dim(embed_weight, lax.axis_index("seq") * shard, shard, 1)
    folded = lax.psum(jnp.dot(mine, qkv_weight, preferred_element_type=F32), "seq")
    arrived = lax.all_to_all(
        outgoing.reshape(loaders, capacity, -1), "dp", split_axis=0, concat_axis=0, tiled=True
    ).reshape(slots, -1)
    gathered = lax.all_gather(arrived, "seq", axis=0, tiled=True)
    tokens = 4 * slots
    keys = 4 * gathered.shape[0]
    attended, grad = pl.pallas_call(
        attend_kernel,
        out_shape=(
            jax.ShapeDtypeStruct((tokens, 128), BF16),
            jax.ShapeDtypeStruct((1, 128), F32),
        ),
        scratch_shapes=[
            pltpu.VMEM((keys, 384), BF16),
            pltpu.VMEM((keys, 128), BF16),
            pltpu.VMEM((tokens, keys), F32),
        ],
        compiler_params=pltpu.CompilerParams(vmem_limit_bytes=48 << 20),
    )(arrived, gathered, folded, jnp.tile(rope_freq, 2)[None, :], cotangent)
    freq_grad = lax.psum(grad[0, :64], ("dp", "seq"))
    return attended, freq_grad


def solution(mesh):
    both = ("dp", "seq")
    specs = (
        P(both, None, None, None, None),
        P(both),
        P(both, None),
        P(),
        P(),
        P(),
        P(),
        P(),
        P("seq", None),
        P(),
        P(both, None),
    )
    return jax.shard_map(
        per_device,
        mesh=mesh,
        in_specs=specs,
        out_specs=(P(both, None), P()),
        check_vma=False,
    )
```

profile of v0, /device:TPU:1, one launch (start us, length us, event | category | flops | bytes accessed | tf_op | source)
XLA Modules:
  0.0 280.5 jit_solution(6069288452288844804)
XLA Ops:
  7.2 0.0 copy-start
  7.2 0.0 copy-start.6
  7.2 0.0 copy-start.8
  7.2 0.0 copy-start.7
  7.2 0.0 copy-start.4
  7.2 1.5 copy.26.space_ref
  8.7 1.1 copy.27.time_ref
  9.8 0.0 copy-done.6
  9.8 0.0 copy-start.5
  9.8 0.1 copy.28.latent_ref
  9.9 0.1 convert_reduce_fusion
  10.0 0.1 broadcast_in_dim.7
  10.1 0.1 broadcast_in_dim_reshape.3.slot8_ref
  10.2 0.0 copy-done.7
  10.2 0.1 copy.25
  10.3 0.0 copy-done.4
  10.3 0.0 copy-start.1
  10.4 1.6 copy-done.1
  11.9 4.6 %shard_map.122 = bf16[64,384]{1,0:T(8,128)(2,1)S(1)} custom-call(bf16[32,2,8,8,192]{4,3,2,1,0:T(8,128)(2,1)S(1)} %copy-done.1, bf16[1728,192]{1,0:T(8,128)(2,1)S(1)} %copy.26.space_ref, bf16[576,192]{1,0:T(8,128)(2,1)S(1)} %copy.27.time_ref, f32[1,192]{1,0:T(1,128)S(1)} %bitcast.7, bf16[192,256]{1,0:T(8,128)(2,1)S(1)} %copy.28.latent_ref, ...), custom_call_target="tpu_custom_call" | custom-call | tf_op jit(solution)/shard_map/pallas_call | solution.py:247
  16.6 0.6 reshape.17
  17.2 10.4 %all-to-all-start = ((bf16[32,2,384]{2,1,0:T(2,128)(2,1)}), bf16[32,2,384]{2,1,0:T(2,128)(2,1)S(1)}, u32[]{:S(2)}, u32[]{:S(2)}) async-start(bf16[32,2,384]{2,1,0:T(2,128)(2,1)} %reshape.17), calls=%async_computation | async-start | bytes 98304 | tf_op jit(solution)/shard_map/all_to_all | solution.py:264
  27.6 0.0 all-reduce.4.cloned.1.call-start
  27.7 0.9 fusion
  28.6 0.0 all-reduce.4.cloned.1.call-update
  28.6 0.1 broadcast_in_dim_tile.3.freq_ref
  28.7 6.4 %all-to-all-done = bf16[32,2,384]{2,1,0:T(2,128)(2,1)S(1)} async-done(((bf16[32,2,384]{2,1,0:T(2,128)(2,1)}), bf16[32,2,384]{2,1,0:T(2,128)(2,1)S(1)}, u32[]{:S(2)}, u32[]{:S(2)}) %all-to-all-start) | async-done | bytes 49184 | tf_op jit(solution)/shard_map/all_to_all | solution.py:264
  35.1 31.3 %all_gather.3.all_ref = bf16[1024,384]{1,0:T(8,128)(2,1)S(1)} all-gather(bf16[64,384]{1,0:T(8,128)(2,1)S(1)} %reshape.18.own_ref), channel_id=1, replica_groups=mesh['dp'=32,'seq'=16] {'seq'}, dimensions={0}, use_global_device_ids=true | all-gather | bytes 835584 | tf_op jit(solution)/shard_map/all_gather | solution.py:267
  66.4 91.2 %all-reduce.4.cloned.1.call-done.ew_ref = f32[64,384]{1,0:T(8,128)} async-done(((f32[64,384]{1,0:T(8,128)}), f32[64,384]{1,0:T(8,128)}) %all-reduce.4.cloned.1.call-update) | async-done | bytes 98320 | tf_op jit(solution)/shard_map/psum | solution.py:263
  157.6 0.0 copy-done.3
  157.6 0.9 copy-done.2
  158.5 5.6 %shard_map.123 = (bf16[256,128]{1,0:T(8,128)(2,1)}, f32[1,128]{1,0:T(1,128)S(1)}) custom-call(bf16[64,384]{1,0:T(8,128)(2,1)S(1)} %reshape.18.own_ref, bf16[1024,384]{1,0:T(8,128)(2,1)S(1)} %all_gather.3.all_ref, f32[64,384]{1,0:T(8,128)S(1)} %copy-done.2, f32[1,128]{1,0:T(1,128)S(1)} %broadcast_in_dim_tile.3.freq_ref, bf16[256,128]{1,0:T(8,128)(2,1)S(1)} %copy-done.3), custom_call_target="tpu_custom_call" | custom-call | tf_op jit(solution)/shard_map/pallas_call | solution.py:270
  164.1 109.5 %psum.15 = f32[64]{0:T(128)} all-reduce(f32[64]{0:T(128)S(1)} %slice_bitcast_fusion), channel_id=1, replica_groups=mesh['dp'=32,'seq'=16] {'dp','seq'}, use_global_device_ids=true, to_apply=%region_2.3 | all-reduce | flops 64 | bytes 512 | tf_op jit(solution)/shard_map/psum | solution.py:283
  (14 shorter events, 0.1 us)
Async XLA Ops:
  7.2 20.5 %copy-start = (bf16[64,5120]{1,0:T(8,128)(2,1)S(1)}, bf16[64,5120]{1,0:T(8,128)(2,1)}, u32[]{:S(2)}) copy-start(bf16[64,5120]{1,0:T(8,128)(2,1)} %param.18) | copy-start | bytes 1966084
  7.2 2.6 copy-start.6
  7.2 2.7 copy-start.8
  7.2 3.0 %copy-start.7 = (s32[32,4]{0,1:T(4,128)S(1)}, s32[32,4]{0,1:T(4,128)}, u32[]{:S(2)}) copy-start(s32[32,4]{0,1:T(4,128)} %param.13) | copy-start | bytes 1540
  7.2 3.1 %copy-start.4 = (f32[192]{0:T(256)S(1)}, f32[192]{0:T(256)}, u32[]{:S(2)}) copy-start(f32[192]{0:T(256)} %param.16) | copy-start | bytes 2308
  9.8 17.9 %copy-start.5 = (bf16[320,384]{1,0:T(8,128)(2,1)S(1)}, bf16[320,384]{1,0:T(8,128)(2,1)}, u32[]{:S(2)}) copy-start(bf16[320,384]{1,0:T(8,128)(2,1)} %param.19) | copy-start | bytes 737284
  10.1 18.5 %copy-start.9 = (f32[64]{0:T(128)S(1)}, f32[64]{0:T(128)}, u32[]{:S(2)}) copy-start(f32[64]{0:T(128)} %param.20) | copy-start | bytes 772
  10.3 1.6 copy-start.1
  11.9 145.6 %copy-start.3 = (bf16[256,128]{1,0:T(8,128)(2,1)S(1)}, bf16[256,128]{1,0:T(8,128)(2,1)}, u32[]{:S(2)}) copy-start(bf16[256,128]{1,0:T(8,128)(2,1)} %cot_ref.1) | copy-start | bytes 196612
  17.2 17.8 %all-to-all-start = ((bf16[32,2,384]{2,1,0:T(2,128)(2,1)}), bf16[32,2,384]{2,1,0:T(2,128)(2,1)S(1)}, u32[]{:S(2)}, u32[]{:S(2)}) async-start(bf16[32,2,384]{2,1,0:T(2,128)(2,1)} %reshape.17), calls=%async_computation | async-start | bytes 98304 | tf_op jit(solution)/shard_map/all_to_all | solution.py:264
  27.6 130.0 %all-reduce.4.cloned.1.call-start = ((), (), s32[]{:S(2)}) async-start(), calls=%async_computation.1 | async-start | bytes 196608 | tf_op jit(solution)/shard_map/psum | solution.py:263
  157.6 0.9 copy-start.2
Sparse Core Ops, SparseCore 0:
  30.8 126.7 all-reduce.3
where the time goes:
time: 281 us; the launch traced here: 280 us
  blocking collectives  141 us (50%)
  waiting for transfers between devices  97.5 us (35%)
  between operations  14.2 us (5%)
  starting transfers between devices  10.4 us (4%)
  Pallas kernels  10.3 us (4%)
  local copies, waits for them, and re-layouts  6.2 us (2%)
    psum x1, blocking collectives, per_device(): freq_grad = lax.psum(grad[0, :64], ('dp', 'seq'))  110 us
    psum x1, waiting for transfers between devices, per_device(): lax.psum(jnp.dot(mine, qkv_weight, preferred_element_type=F32), 'seq')  91.2 us
    all_gather x1, blocking collectives, per_device(): gathered = lax.all_gather(arrived, 'seq', axis=0, tiled=True)  31.3 us
    all_to_all x1, starting transfers between devices, per_device(): lax.all_to_all(outgoing.reshape(loaders, capacity, -1), 'dp', split_axis=...  10.4 us
    all_to_all x1, waiting for transfers between devices, per_device(): lax.all_to_all(outgoing.reshape(loaders, capacity, -1), 'dp', split_axis=...  6.35 us
    pallas_call x1, Pallas kernels, per_device(): pl.pallas_call(attend_kernel, out_shape=(jax.ShapeDtypeStruct((tokens, 12...  5.64 us
  transfers between devices with their start and end apart: 2, of which 2 were waited for; matrix products, arithmetic and copies ran while one was open for 0% of the time, Pallas kernels for 0%

commit v1 on v0

v1 whole, which is shorter than its diff:
```python
import math

import jax
import jax.numpy as jnp
from jax import lax
from jax.experimental import pallas as pl
from jax.experimental.pallas import tpu as pltpu
from jax.sharding import PartitionSpec as P

F32 = jnp.float32
BF16 = jnp.bfloat16
MESH = pl.DeviceIdType.MESH
META = 128
BIG = 1e30
UNITS = 24
FIELDS = 16


def iota(shape, dim):
    return lax.broadcasted_iota(jnp.int32, shape, dim)


def dot(a, b):
    return jnp.dot(a, b, preferred_element_type=F32)


def dot_nt(a, b):
    return lax.dot_general(a, b, (((1,), (1,)), ((), ())), preferred_element_type=F32)


def dot_tn(a, b):
    return lax.dot_general(a, b, (((0,), (0,)), ((), ())), preferred_element_type=F32)


def one_hot(cond):
    return jnp.where(cond, 1.0, 0.0).astype(BF16)


def encode_rows(h, tiles_ref, space_ref, time_ref, bias_ref, latent_ref):
    held, frames, height, width, chans = tiles_ref.shape
    rows = held * width
    lat_wide = latent_ref.shape[1]
    shifted = [None, None, None]
    for row_off in range(3):
        src = 2 * h + row_off
        if src >= height:
            continue
        x = tiles_ref[:, :, src].reshape(held * frames * width, chans)
        for col_off in range(3):
            tap = (row_off * 3 + col_off) * chans
            part = dot(x, space_ref[tap : tap + chans, :])
            old = shifted[col_off]
            shifted[col_off] = part if old is None else old + part
    y0, y1, y2 = [y.reshape(held * frames, width, chans) for y in shifted]
    y1 = pltpu.roll(y1, width - 1, axis=1)
    edge = iota((1, width, chans), 1) < width - 2
    y2 = jnp.where(edge, pltpu.roll(y2, width - 2, axis=1), 0.0)
    spatial = (y0 + y1 + y2).reshape(held, frames, width, chans)
    first = spatial[:, 0].reshape(rows, chans).astype(BF16)
    second = spatial[:, 1].reshape(rows, chans).astype(BF16)
    summed = dot(first, time_ref[chans : 2 * chans, :]) + dot(second, time_ref[2 * chans :, :])
    summed = summed + bias_ref[...]
    feats = (summed / (1.0 + jnp.exp(-summed))).astype(BF16)
    lane = iota((rows, lat_wide), 1)
    lane_h = 2 * (lane // 128) + (lane // 32) % 2
    lane_w = 2 * ((lane // 64) % 2) + (lane // 16) % 2
    keep = (lane_h == h) & (2 * lane_w == iota((rows, lat_wide), 0) % width)
    return jnp.where(keep, dot(feats, latent_ref[...]), 0.0)


def pack_messages(latents, slot8_ref, slot_ref, meta_ref, out_ref):
    owners = out_ref.shape[0]
    rows = latents.shape[0]
    held = meta_ref.shape[0]
    latents = latents.astype(BF16)
    shape = (8 * owners, rows)
    sub = iota(shape, 0) % 8
    hit = (2 * (iota(shape, 0) // 8) + sub // 2 == slot8_ref[...]) & (sub < 4)
    packed = dot(one_hot(hit & (sub % 2 == 0)), latents[:, 0:128])
    packed = packed + dot(one_hot(hit & (sub % 2 == 1)), latents[:, 128:256])
    shape = (8 * owners, held)
    hit = (iota(shape, 0) // 8 == slot_ref[...] // 2) & (iota(shape, 0) % 8 == 4)
    packed = packed + dot(one_hot(hit), meta_ref[...])
    out_ref[...] = packed.astype(BF16).reshape(owners, 8, 128)


def unpack_messages(arrived, block_ref, mine):
    loaders = arrived.shape[0]
    slots = 2 * loaders
    flat = arrived.reshape(8 * loaders, 128)
    shape = (slots, 8 * loaders)
    base = 8 * (iota(shape, 0) // 2) + 2 * (iota(shape, 0) % 2)
    block_ref[mine, 0:slots, 0:128] = dot(one_hot(iota(shape, 1) == base), flat).astype(BF16)
    block_ref[mine, 0:slots, 128:256] = dot(one_hot(iota(shape, 1) == base + 1), flat).astype(BF16)
    both = dot(one_hot(iota(shape, 1) == 8 * (iota(shape, 0) // 2) + 4), flat)
    odd = iota((slots, META), 0) % 2 == 1
    fields = jnp.where(odd, pltpu.roll(both, META - 8, axis=1), both)
    pick = one_hot((iota((FIELDS, META), 0) == iota((FIELDS, META), 1)) & (iota((FIELDS, META), 1) < 8))
    turned = dot_nt(pick, fields.astype(BF16)).astype(BF16)
    wide = jnp.concatenate([turned, jnp.zeros((FIELDS, 256 - slots), BF16)], axis=1)
    block_ref[mine, slots : slots + FIELDS, :] = wide


def sincos(angle):
    turns = jnp.floor(angle * (0.5 / math.pi) + 0.5)
    r = angle - turns * 6.28125
    r = r - turns * (2.0 * math.pi - 6.28125)
    z = r * r
    s = jnp.full_like(z, -1.0 / math.factorial(15))
    for n in (13, 11, 9, 7, 5, 3, 1):
        s = s * z + (1.0 if n % 4 == 1 else -1.0) / math.factorial(n)
    c = jnp.full_like(z, 1.0 / math.factorial(16))
    for n in (14, 12, 10, 8, 6, 4, 2, 0):
        c = c * z + (1.0 if n % 4 == 0 else -1.0) / math.factorial(n)
    return s * r, c


def axis_masks(shape):
    pair = iota(shape, 1) % 64
    return pair < 22, (pair >= 22) & (pair < 43), pair >= 43


def swap_halves(u):
    lane = iota(u.shape, 1)
    turned = pltpu.roll(u, 64, axis=1)
    return jnp.where(lane < 64, -turned, turned)


def rotary_tables(freq):
    shape = (FIELDS, META)
    sub = iota(shape, 0)
    in_f, in_r, in_c = axis_masks(shape)
    step = jnp.where((sub == 1) & in_f, 1.0, 0.0)
    step = jnp.where(((sub == 2) & in_r) | ((sub == 3) & in_c), 2.0, step)
    rest = jnp.broadcast_to(freq, shape)
    tables = []
    for _ in range(3):
        part = rest.astype(BF16).astype(F32)
        rest = rest - part
        tables.append((step * part).astype(BF16))
    return jnp.concatenate(tables + [step.astype(BF16)], axis=1)


def token_weights(ew_ref, freq, first):
    base = ew_ref[:, first : first + 128]
    shape = (8, 128)
    in_f, in_r, in_c = axis_masks(shape)
    blocks = []
    for tok in range(4):
        offset = jnp.where(in_r, float(tok // 2), 0.0) + jnp.where(in_c, float(tok % 2), 0.0)
        s, c = sincos(jnp.broadcast_to(freq, shape) * offset)
        turned = base * c[0:1, :] + swap_halves(base) * s[0:1, :]
        blocks.append(jnp.concatenate([turned, swap_halves(turned)], axis=1))
    return jnp.concatenate(blocks, axis=0).astype(BF16)


def from_fields(fields, tables):
    wide = dot_tn(fields, tables)
    angle = wide[:, 0:128] + wide[:, 128:256] + wide[:, 256:384]
    s, c = sincos(angle)
    return s, c, wide[:, 384:512]


def project_keys(lat, fields, tables, wk, wv, keys_ref, vals_ref, at):
    slots = lat.shape[0]
    tokens = 4 * slots
    s, c, pos = from_fields(fields, tables)
    which = iota((tokens, 256), 0) // slots == iota((tokens, 256), 1) // 64
    spread = jnp.where(which, jnp.concatenate([lat.astype(F32)] * 4, axis=0), 0.0).astype(BF16)
    u = dot(spread, wk)
    tok = iota((tokens, 128), 0) // slots
    in_f, in_r, in_c = axis_masks((tokens, 128))
    shift = jnp.where(in_r & (tok >= 2), 1.0, 0.0) + jnp.where(in_c & (tok % 2 == 1), 1.0, 0.0)
    k = u[:, 0:128] * jnp.concatenate([c] * 4, axis=0) + u[:, 128:256] * jnp.concatenate([s] * 4, axis=0)
    pick = one_hot((iota((FIELDS, META), 0) == 4) & (iota((FIELDS, META), 1) == 0))
    dead = jnp.where(iota((slots, META), 1) == 0, (dot_tn(fields, pick) - 1.0) * BIG, 0.0).astype(BF16)
    keys_ref[pl.ds(at, tokens), 0:128] = jnp.concatenate([dead] * 4, axis=0)
    keys_ref[pl.ds(at, tokens), 128:256] = k.astype(BF16)
    keys_ref[pl.ds(at, tokens), 256:384] = (k * (jnp.concatenate([pos] * 4, axis=0) + shift)).astype(BF16)
    vals_ref[pl.ds(at, tokens), :] = dot(spread, wv).astype(BF16)


def project_queries(lat, fields, tables, wq):
    slots = lat.shape[0]
    tokens = 4 * slots
    taken = (iota((tokens, slots), 0) // 4).astype(F32) == fields[0:1, :].astype(F32)
    chosen = one_hot(taken & (fields[4:5, :].astype(F32) > 0.5))
    which = iota((tokens, 256), 0) % 4 == iota((tokens, 256), 1) // 64
    my_lat = jnp.where(which, dot(chosen, lat), 0.0).astype(BF16)
    my_fields = dot_nt(fields, chosen).astype(BF16)
    s, c, pos = from_fields(my_fields, tables)
    pick = one_hot(iota((FIELDS, META), 0) == 4)
    live = dot_tn(my_fields, pick)
    u = dot(my_lat, wq)
    q = u[:, 0:128] * c + u[:, 128:256] * s
    in_f, in_r, in_c = axis_masks((tokens, 128))
    tok = iota((tokens, 128), 0) % 4
    pos = pos + jnp.where(in_r & (tok >= 2), 1.0, 0.0) + jnp.where(in_c & (tok % 2 == 1), 1.0, 0.0)
    lane0 = one_hot(iota((tokens, META), 1) == 0)
    scale = 128.0 ** (-0.5) * math.log2(math.e)
    q_ext = jnp.concatenate([lane0, (q * scale).astype(BF16)], axis=1)
    return q, q_ext, pos, live


def finish_attention(q, q_ext, pos, live, top, cot_ref, out_ref, keys_ref, vals_ref, score_ref):
    tokens = q.shape[0]
    keys = keys_ref.shape[0]
    chunk = min(512, keys)
    starts = range(0, keys, chunk)
    top = jnp.max(top, axis=1, keepdims=True)
    sums = jnp.zeros((tokens, chunk), F32)
    mixed = jnp.zeros((tokens, 128), F32)
    for at in starts:
        weights = jnp.exp2(score_ref[:, at : at + chunk] - top)
        score_ref[:, at : at + chunk] = weights
        sums = sums + weights
        mixed = mixed + dot(weights.astype(BF16), vals_ref[at : at + chunk, :])
    inv = 1.0 / jnp.sum(sums, axis=1, keepdims=True)
    mixed = mixed * inv
    out_ref[...] = (mixed * live).astype(BF16)
    cot = cot_ref[...]
    mean = jnp.sum(cot.astype(F32) * mixed, axis=1, keepdims=True)
    back = jnp.zeros((tokens, 256), F32)
    for at in starts:
        dprob = dot_nt(cot, vals_ref[at : at + chunk, :])
        dscore = score_ref[:, at : at + chunk] * (dprob - mean)
        back = back + dot(dscore.astype(BF16), keys_ref[at : at + chunk, 128:384])
    g = pltpu.roll(back[:, 0:128], 64, axis=1)
    gp = pltpu.roll(back[:, 128:256], 64, axis=1)
    terms = q * (pos * g - gp) * (inv * 128.0 ** (-0.5) * live)
    line = jnp.sum(terms, axis=0, keepdims=True)
    other = pltpu.roll(line, 64, axis=1)
    return jnp.where(iota((1, 128), 1) < 64, line - other, other - line)


def greet():
    me_dp, me_seq = lax.axis_index("dp"), lax.axis_index("seq")
    n_dp, n_seq = lax.axis_size("dp"), lax.axis_size("seq")
    barrier = pltpu.get_barrier_semaphore()

    def to_dp(i, _):
        peer = lax.rem(me_dp + i, n_dp)
        pl.semaphore_signal(barrier, inc=1, device_id=(peer, me_seq), device_id_type=MESH)
        return 0

    def to_seq(i, _):
        peer = lax.rem(me_seq + i, n_seq)
        pl.semaphore_signal(barrier, inc=1, device_id=(me_dp, peer), device_id_type=MESH)
        return 0

    lax.fori_loop(1, n_dp, to_dp, 0)
    lax.fori_loop(1, n_seq, to_seq, 0)
    return barrier, n_dp + n_seq - 2


def spread(axis, src_of, dst_ref, send_sem, recv_sem):
    me_dp, me_seq = lax.axis_index("dp"), lax.axis_index("seq")
    n = lax.axis_size(axis)
    me = lax.axis_index(axis)

    def copy(peer, slot):
        where = (peer, me_seq) if axis == "dp" else (me_dp, peer)
        return pltpu.make_async_remote_copy(
            src_ref=src_of(peer),
            dst_ref=dst_ref.at[slot],
            send_sem=send_sem.at[peer],
            recv_sem=recv_sem.at[slot],
            device_id=where,
            device_id_type=MESH,
        )

    def each(act):
        def body(i, _):
            act(lax.rem(me + i, n))
            return 0

        lax.fori_loop(1, n, body, 0)

    def start():
        each(lambda peer: copy(peer, me).start())

    def wait_recv():
        each(lambda peer: copy(peer, peer).wait_recv())

    def wait_send():
        each(lambda peer: copy(peer, me).wait_send())

    return start, wait_recv, wait_send


def fold_partial(embed_ref, qkv_ref, unit, window, sem):
    shard = qkv_ref.shape[0]
    wide = window.shape[1]
    me_seq = lax.axis_index("seq")
    first = (me_seq * shard) // 128 * 128
    rows = pl.ds(pl.multiple_of(8 * (unit // 3), 8), 8)
    load = pltpu.make_async_copy(embed_ref.at[rows, pl.ds(pl.multiple_of(first, 128), wide)], window, sem)
    load.start()
    load.wait()
    part = window[...].astype(F32)
    if wide != shard:
        part = jnp.where(me_seq % 2 == 1, pltpu.roll(part, wide - 64, axis=1), part)
    cols = pl.ds(pl.multiple_of(128 * (unit % 3), 128), 128)
    return dot(part[:, 0:shard].astype(BF16), qkv_ref[:, cols])


def gather_kernel(
    out_ref,
    embed_ref,
    qkv_ref,
    block_ref,
    ew_ref,
    window,
    load_sem,
    parts,
    unit_buf,
    unit_all,
    arrived,
    part_send,
    part_recv,
    unit_send,
    unit_recv,
    msg_send,
    msg_recv,
    ring_send,
    ring_recv,
):
    me_dp, me_seq = lax.axis_index("dp"), lax.axis_index("seq")
    n_dp, n_seq = lax.axis_size("dp"), lax.axis_size("seq")
    barrier, count = greet()
    per = parts.shape[1]
    for j in range(per):
        unit = lax.rem(me_dp * per + j, UNITS)
        parts[me_seq, j] = fold_partial(embed_ref, qkv_ref, unit, window, load_sem)
    pl.semaphore_wait(barrier, count)

    start_parts, recv_parts, sent_parts = spread("seq", lambda peer: parts.at[me_seq], parts, part_send, part_recv)
    start_msgs, recv_msgs, sent_msgs = spread("dp", lambda peer: out_ref.at[peer], arrived, msg_send, msg_recv)
    start_units, recv_units, sent_units = spread("dp", lambda peer: unit_buf, unit_all, unit_send, unit_recv)

    start_msgs()
    start_parts()
    arrived[me_dp] = out_ref[me_dp]
    recv_msgs()
    unpack_messages(arrived[...], block_ref, me_seq)

    right, left = lax.rem(me_seq + 1, n_seq), lax.rem(me_seq + n_seq - 1, n_seq)

    def hop(owner, to, way):
        return pltpu.make_async_remote_copy(
            src_ref=block_ref.at[owner],
            dst_ref=block_ref.at[owner],
            send_sem=ring_send.at[way, owner],
            recv_sem=ring_recv.at[owner],
            device_id=(me_dp, to),
            device_id_type=MESH,
        )

    far_right, far_left = n_seq // 2, (n_seq - 1) // 2
    hop(me_seq, right, 0).start()
    if far_left:
        hop(me_seq, left, 1).start()

    recv_parts()
    unit_buf[...] = jnp.sum(parts[...], axis=0)
    unit_all[me_dp] = unit_buf[...]
    start_units()

    def step(t, _):
        owner = lax.rem(me_seq + n_seq - t, n_seq)
        hop(owner, right, 0).wait_recv()

        @pl.when(t < far_right)
        def _():
            hop(owner, right, 0).start()

        @pl.when(t <= far_left)
        def _():
            owner = lax.rem(me_seq + t, n_seq)
            hop(owner, left, 1).wait_recv()

            @pl.when(t < far_left)
            def _():
                hop(owner, left, 1).start()

        return 0

    lax.fori_loop(1, far_right + 1, step, 0)
    recv_units()
    for unit in range(UNITS):
        ew_ref[8 * (unit // 3) : 8 * (unit // 3) + 8, 128 * (unit % 3) : 128 * (unit % 3) + 128] = unit_all[unit // per, unit % per]

    def drain(t, _):
        hop(lax.rem(me_seq + n_seq - t, n_seq), right, 0).wait_send()

        @pl.when(t < far_left)
        def _():
            hop(lax.rem(me_seq + t, n_seq), left, 1).wait_send()

        return 0

    lax.fori_loop(0, far_right, drain, 0)
    sent_msgs()
    sent_parts()
    sent_units()


def attend_kernel(block_ref, ew_ref, freq_ref, cot_ref, out_ref, grad_ref, keys_ref, vals_ref, score_ref):
    n_seq, rows, _ = block_ref.shape
    slots = rows - FIELDS
    tokens = 4 * slots
    freq = freq_ref[...]
    tables = rotary_tables(freq)
    me_seq = lax.axis_index("seq")
    wq = token_weights(ew_ref, freq, 0)
    wk = token_weights(ew_ref, freq, 128)
    wv = jnp.concatenate([ew_ref[:, 256:384]] * 4, axis=0).astype(BF16)
    mine = block_ref.at[me_seq]
    q, q_ext, pos, live = project_queries(mine[0:slots, :], mine[slots:, 0:slots], tables, wq)

    def step(i, top):
        at = pl.multiple_of(i * tokens, tokens)
        block = block_ref.at[i]
        project_keys(block[0:slots, :], block[slots:, 0:slots], tables, wk, wv, keys_ref, vals_ref, at)
        scores = dot_nt(q_ext, keys_ref[pl.ds(at, tokens), 0:256])
        score_ref[:, pl.ds(at, tokens)] = scores
        return jnp.maximum(top, scores)

    top = lax.fori_loop(0, n_seq, step, jnp.full((tokens, tokens), -jnp.inf, F32))
    grad_ref[...] = finish_attention(q, q_ext, pos, live, top, cot_ref, out_ref, keys_ref, vals_ref, score_ref)


def sum_kernel(line_ref, out_ref, by_seq, by_dp, mid, seq_send, seq_recv, dp_send, dp_recv):
    me_dp, me_seq = lax.axis_index("dp"), lax.axis_index("seq")
    barrier, count = greet()
    by_seq[me_seq] = line_ref[...]
    pl.semaphore_wait(barrier, count)
    start, recv, sent = spread("seq", lambda peer: line_ref, by_seq, seq_send, seq_recv)
    start()
    recv()
    mid[...] = jnp.sum(by_seq[...], axis=0)
    by_dp[me_dp] = mid[...]
    start2, recv2, sent2 = spread("dp", lambda peer: mid, by_dp, dp_send, dp_recv)
    start2()
    recv2()
    out_ref[...] = jnp.sum(by_dp[...], axis=0)
    sent()
    sent2()


def per_device(
    tiles,
    tile_dest,
    tile_meta,
    space_weight,
    time_weight,
    conv_bias,
    latent_weight,
    embed_weight,
    qkv_weight,
    rope_freq,
    cotangent,
):
    n_dp, n_seq = lax.axis_size("dp"), lax.axis_size("seq")
    held = tiles.shape[0]
    slots = 2 * n_dp
    tokens = 4 * slots
    keys = tokens * n_seq
    per = -(-UNITS // n_dp)
    order = jnp.arange(held, dtype=jnp.int32)
    same = (tile_dest[:, None] == tile_dest[None, :]) & (order[:, None] < order[None, :])
    rank = jnp.sum(same.astype(jnp.int32), axis=0)
    slot = tile_dest * 2 + rank
    meta = jnp.concatenate([tile_meta, jnp.ones((held, 1), jnp.int32)], axis=1)
    meta = jnp.tile(jnp.pad(meta, ((0, 0), (0, 3))), (1, META // 8))
    meta = jnp.where(jnp.arange(META)[None, :] // 8 == rank[:, None], meta, 0).astype(BF16)

    def encode_kernel(tiles_ref, space_ref, time_ref, bias_ref, latent_ref, slot8_ref, slot_ref, meta_ref, out_ref):
        total = None
        for h in range(tiles_ref.shape[2] // 2):
            part = encode_rows(h, tiles_ref, space_ref, time_ref, bias_ref, latent_ref)
            total = part if total is None else total + part
        pack_messages(total, slot8_ref, slot_ref, meta_ref, out_ref)

    outgoing = pl.pallas_call(
        encode_kernel,
        out_shape=jax.ShapeDtypeStruct((n_dp, 8, 128), BF16),
        compiler_params=pltpu.CompilerParams(vmem_limit_bytes=48 << 20),
    )(
        tiles,
        space_weight,
        time_weight,
        conv_bias[None, :],
        jnp.tile(latent_weight, (1, 16)),
        jnp.repeat(slot, tiles.shape[3])[None, :],
        slot[None, :],
        meta,
    )
    shard = qkv_weight.shape[0]
    vmem = pl.BlockSpec(memory_space=pltpu.VMEM)
    dma = pltpu.SemaphoreType.DMA
    blocks, folded = pl.pallas_call(
        gather_kernel,
        out_shape=(
            jax.ShapeDtypeStruct((n_seq, slots + FIELDS, 256), BF16),
            jax.ShapeDtypeStruct((64, 384), F32),
        ),
        in_specs=[vmem, pl.BlockSpec(memory_space=pl.ANY), vmem],
        out_specs=(vmem, vmem),
        scratch_shapes=[
            pltpu.VMEM((8, -(-shard // 128) * 128), BF16),
            dma(()),
            pltpu.VMEM((n_seq, per, 8, 128), F32),
            pltpu.VMEM((per, 8, 128), F32),
            pltpu.VMEM((n_dp, per, 8, 128), F32),
            pltpu.VMEM((n_dp, 8, 128), BF16),
            dma((n_seq,)),
            dma((n_seq,)),
            dma((n_dp,)),
            dma((n_dp,)),
            dma((n_dp,)),
            dma((n_dp,)),
            dma((2, n_seq)),
            dma((n_seq,)),
        ],
        compiler_params=pltpu.CompilerParams(
            vmem_limit_bytes=32 << 20, collective_id=0, has_side_effects=True
        ),
    )(outgoing, embed_weight, qkv_weight)
    attended, grad = pl.pallas_call(
        attend_kernel,
        out_shape=(
            jax.ShapeDtypeStruct((tokens, 128), BF16),
            jax.ShapeDtypeStruct((1, 128), F32),
        ),
        scratch_shapes=[
            pltpu.VMEM((keys, 384), BF16),
            pltpu.VMEM((keys, 128), BF16),
            pltpu.VMEM((tokens, keys), F32),
        ],
        compiler_params=pltpu.CompilerParams(vmem_limit_bytes=48 << 20),
    )(blocks, folded, jnp.tile(rope_freq, 2)[None, :], cotangent)
    summed = pl.pallas_call(
        sum_kernel,
        out_shape=jax.ShapeDtypeStruct((1, 128), F32),
        in_specs=[vmem],
        out_specs=vmem,
        scratch_shapes=[
            pltpu.VMEM((n_seq, 1, 128), F32),
            pltpu.VMEM((n_dp, 1, 128), F32),
            pltpu.VMEM((1, 128), F32),
            dma((n_seq,)),
            dma((n_seq,)),
            dma((n_dp,)),
            dma((n_dp,)),
        ],
        compiler_params=pltpu.CompilerParams(
            vmem_limit_bytes=32 << 20, collective_id=1, has_side_effects=True
        ),
    )(grad)
    return attended, summed[0, :64]


def solution(mesh):
    both = ("dp", "seq")
    specs = (
        P(both, None, None, None, None),
        P(both),
        P(both, None),
        P(),
        P(),
        P(),
        P(),
        P(),
        P("seq", None),
        P(),
        P(both, None),
    )
    return jax.shard_map(
        per_device,
        mesh=mesh,
        in_specs=specs,
        out_specs=(P(both, None), P()),
        check_vma=False,
    )
```

time: 281 us -> 95.9 us (0.34)
  blocking collectives: 141 us -> 0 us
  waiting for transfers between devices: 97.5 us -> 0 us
  Pallas kernels: 10.3 us -> 87.7 us
  between operations: 14.2 us -> 0.77 us
  starting transfers between devices: 10.4 us -> 0 us
    psum x1 -> x0, blocking collectives: 110 us -> none  [per_device(): freq_grad = lax.psum(grad[0, :64], ('dp', 'seq'))]
    psum x1 -> x0, waiting for transfers between devices: 91.2 us -> none  [per_device(): lax.psum(jnp.dot(mine, qkv_weight, preferred_element_type=F32), 'seq')]
    pallas_call x1 -> x3, Pallas kernels: 4.64 us -> 76.3 us  [the longest x1 45.5 us: per_device(): pl.pallas_call(gather_kernel, out_shape=(jax.ShapeDtypeStruct((n_seq, slo...]
    all_gather x1 -> x0, blocking collectives: 31.3 us -> none  [per_device(): gathered = lax.all_gather(arrived, 'seq', axis=0, tiled=True)]
    all_to_all x1 -> x0, starting transfers between devices: 10.4 us -> none  [per_device(): lax.all_to_all(outgoing.reshape(loaders, capacity, -1), 'dp', split_axis=...]
    all_to_all x1 -> x0, waiting for transfers between devices: 6.35 us -> none  [per_device(): lax.all_to_all(outgoing.reshape(loaders, capacity, -1), 'dp', split_axis=...]
    pallas_call x1, Pallas kernels: 5.64 us -> 11.4 us  [per_device(): pl.pallas_call(attend_kernel, out_shape=(jax.ShapeDtypeStruct((tokens, 12...]
  transfers between devices with their start and end apart: 2 -> 0, of which waited for: 2 -> 0; matrix products, arithmetic and copies ran while one was open for 0% -> 0% of each run, Pallas kernels for 0% -> 0%
where the time goes in v1:
time: 95.9 us; the launch traced here: 95.6 us
  Pallas kernels  87.7 us (91%)
  local copies, waits for them, and re-layouts  4.83 us (5%)
  other arithmetic  2.33 us (2%)
    pallas_call x1, Pallas kernels, per_device(): pl.pallas_call(gather_kernel, out_shape=(jax.ShapeDtypeStruct((n_seq, slo...  45.5 us
    pallas_call x1, Pallas kernels, per_device(): pl.pallas_call(sum_kernel, out_shape=jax.ShapeDtypeStruct((1, 128), F32),...  26 us
    pallas_call x1, Pallas kernels, per_device(): pl.pallas_call(attend_kernel, out_shape=(jax.ShapeDtypeStruct((tokens, 12...  11.4 us
    pallas_call x1, Pallas kernels, per_device(): pl.pallas_call(encode_kernel, out_shape=jax.ShapeDtypeStruct((n_dp, 8, 12...  4.8 us
    unnamed x12, local copies, waits for them, and re-layouts  2.53 us

profile of v1, /device:TPU:1, one launch (start us, length us, event | category | flops | bytes accessed | tf_op | source)
XLA Modules:
  0.0 95.6 jit_solution(14476580553440659240)
XLA Ops:
  0.6 0.0 copy-start.4
  0.6 0.0 copy-start
  0.6 0.9 convert_reduce_fusion
  1.6 0.7 multiply_add_fusion
  2.2 0.7 tile.28
  2.9 0.1 broadcast_in_dim_tile.3.freq_ref
  3.0 0.7 pad_select_fusion
  3.6 0.1 broadcast_in_dim.11
  3.7 0.1 broadcast_in_dim_reshape.3.slot8_ref
  3.8 0.1 copy.21
  3.9 0.1 select_convert_fusion.meta_ref
  4.0 0.7 tile.10
  4.7 0.1 copy.24.latent_ref
  4.8 1.1 %copy.23.time_ref = bf16[576,192]{1,0:T(8,128)(2,1)S(1)} copy(bf16[576,192]{0,1:T(8,128)(2,1)} %param.15) | data formatting | bytes 442368 | tf_op args[4]
  5.9 1.4 %copy.22.space_ref = bf16[1728,192]{1,0:T(8,128)(2,1)S(1)} copy(bf16[1728,192]{0,1:T(8,128)(2,1)} %param.14) | data formatting | bytes 1327104 | tf_op args[3]
  7.3 0.0 copy-done.4
  7.3 0.0 copy-done
  7.3 0.0 copy-start.1
  7.3 0.0 copy-start.2
  7.3 0.0 copy-start.3
  7.4 4.8 %shard_map.122.out_ref = bf16[32,8,128]{2,1,0:T(8,128)(2,1)S(1)} custom-call(bf16[32,2,8,8,192]{4,3,2,1,0:T(8,128)(2,1)S(1)} %copy-done, bf16[1728,192]{1,0:T(8,128)(2,1)S(1)} %copy.22.space_ref, bf16[576,192]{1,0:T(8,128)(2,1)S(1)} %copy.23.time_ref, f32[1,192]{1,0:T(1,128)S(1)} %bitcast.8, bf16[192,256]{1,0:T(8,128)(2,1)S(1)} %copy.24.latent_ref, ...), custom_call_target="tpu_custom_call" | custom-call | tf_op jit(solution)/shard_map/pallas_call | solution.py:485
  12.2 0.0 copy-done.1
  12.2 0.0 copy-done.2
  12.2 45.5 %shard_map.123 = (bf16[16,80,256]{2,1,0:T(8,128)(2,1)S(1)}, f32[64,384]{1,0:T(8,128)S(1)}) custom-call(bf16[32,8,128]{2,1,0:T(8,128)(2,1)S(1)} %shard_map.122.out_ref, bf16[64,5120]{1,0:T(8,128)(2,1)S(1)} %copy-done.1, bf16[320,384]{1,0:T(8,128)(2,1)S(1)} %copy-done.2), custom_call_target="tpu_custom_call" | custom-call | tf_op jit(solution)/shard_map/pallas_call | solution.py:502
  57.6 0.0 copy-done.3
  57.7 11.4 %shard_map.124 = (bf16[256,128]{1,0:T(8,128)(2,1)}, f32[1,128]{1,0:T(1,128)S(1)}) custom-call(bf16[16,80,256]{2,1,0:T(8,128)(2,1)S(1)} %get-tuple-element.6.block_ref, f32[64,384]{1,0:T(8,128)S(1)} %get-tuple-element.7.ew_ref, f32[1,128]{1,0:T(1,128)S(1)} %broadcast_in_dim_tile.3.freq_ref, bf16[256,128]{1,0:T(8,128)(2,1)S(1)} %copy-done.3), custom_call_target="tpu_custom_call" | custom-call | tf_op jit(solution)/shard_map/pallas_call | solution.py:530
  69.1 26.0 %shard_map.125 = f32[1,128]{1,0:T(1,128)S(1)} custom-call(f32[1,128]{1,0:T(1,128)S(1)} %get-tuple-element.9.line_ref), custom_call_target="tpu_custom_call" | custom-call | tf_op jit(solution)/shard_map/pallas_call | solution.py:543
  95.1 0.5 slice_bitcast_fusion
  (2 shorter events, 0.0 us)
Async XLA Ops:
  0.6 6.7 %copy-start.4 = (f32[192]{0:T(256)S(1)}, f32[192]{0:T(256)}, u32[]{:S(2)}) copy-start(f32[192]{0:T(256)} %param.16) | copy-start | bytes 2308
  0.6 6.7 %copy-start = (bf16[32,2,8,8,192]{4,3,2,1,0:T(8,128)(2,1)S(1)}, bf16[32,2,8,8,192]{4,3,2,1,0:T(8,128)(2,1)}, u32[]{:S(2)}) copy-start(bf16[32,2,8,8,192]{4,3,2,1,0:T(8,128)(2,1)} %tiles_ref.1) | copy-start | bytes 4718596
  7.3 4.8 %copy-start.1 = (bf16[64,5120]{1,0:T(8,128)(2,1)S(1)}, bf16[64,5120]{1,0:T(8,128)(2,1)}, u32[]{:S(2)}) copy-start(bf16[64,5120]{1,0:T(8,128)(2,1)} %embed_ref.1) | copy-start | bytes 1966084
  7.3 4.8 %copy-start.2 = (bf16[320,384]{1,0:T(8,128)(2,1)S(1)}, bf16[320,384]{1,0:T(8,128)(2,1)}, u32[]{:S(2)}) copy-start(bf16[320,384]{1,0:T(8,128)(2,1)} %qkv_ref.1) | copy-start | bytes 737284
  7.3 50.3 %copy-start.3 = (bf16[256,128]{1,0:T(8,128)(2,1)S(1)}, bf16[256,128]{1,0:T(8,128)(2,1)}, u32[]{:S(2)}) copy-start(bf16[256,128]{1,0:T(8,128)(2,1)} %cot_ref.1) | copy-start | bytes 196612

commit v2 on v1

v2 whole, which is shorter than its diff:
```python
import math

import jax
import jax.numpy as jnp
from jax import lax
from jax.experimental import pallas as pl
from jax.experimental.pallas import tpu as pltpu
from jax.sharding import PartitionSpec as P

F32 = jnp.float32
BF16 = jnp.bfloat16
MESH = pl.DeviceIdType.MESH
META = 128
BIG = 1e30
UNITS = 24
FIELDS = 8


def iota(shape, dim):
    return lax.broadcasted_iota(jnp.int32, shape, dim)


def dot(a, b):
    return jnp.dot(a, b, preferred_element_type=F32)


def dot_nt(a, b):
    return lax.dot_general(a, b, (((1,), (1,)), ((), ())), preferred_element_type=F32)


def dot_tn(a, b):
    return lax.dot_general(a, b, (((0,), (0,)), ((), ())), preferred_element_type=F32)


def one_hot(cond):
    return jnp.where(cond, 1.0, 0.0).astype(BF16)


def place_tiles(dest_ref, meta_ref, owners):
    held = dest_ref.shape[1]
    square = (held, held)
    row = jnp.broadcast_to(dest_ref[...].astype(F32), square)
    first, second = iota(square, 0), iota(square, 1)
    col = jnp.sum(jnp.where(first == second, row, 0.0), axis=1, keepdims=True)
    same = jnp.where(col == row, 1.0, 0.0)
    rank_row = jnp.sum(jnp.where(first < second, same, 0.0), axis=0, keepdims=True)
    rank_col = jnp.sum(jnp.where(second < first, same, 0.0), axis=1, keepdims=True)
    slot_row = 2.0 * row[0:1, :] + rank_row
    shape = (8, held)
    fields = jnp.concatenate([meta_ref[...].astype(F32), jnp.ones((4, held), F32)], axis=0)
    fields = jnp.where(iota(shape, 0) < 5, fields, 0.0).astype(BF16)
    pick = one_hot(iota((8, META), 0) == iota((8, META), 1) % 8)
    lanes = dot_tn(fields, pick)
    ranked = jnp.where((iota((held, META), 1) // 8).astype(F32) == rank_col, lanes, 0.0).astype(BF16)
    return slot_row, ranked


def encode_rows(h, tiles_ref, space_ref, time_ref, bias, latent):
    held, frames, height, width, chans = tiles_ref.shape
    rows = held * width
    lat_wide = latent.shape[0]
    shifted = [None, None, None]
    for row_off in range(3):
        src = 2 * h + row_off
        if src >= height:
            continue
        x = tiles_ref[:, :, src].reshape(held * frames * width, chans)
        for col_off in range(3):
            part = dot(x, space_ref[row_off * 3 + col_off])
            old = shifted[col_off]
            shifted[col_off] = part if old is None else old + part
    y0, y1, y2 = [y.reshape(held * frames, width, chans) for y in shifted]
    y1 = pltpu.roll(y1, width - 1, axis=1)
    edge = iota((1, width, chans), 1) < width - 2
    y2 = jnp.where(edge, pltpu.roll(y2, width - 2, axis=1), 0.0)
    spatial = (y0 + y1 + y2).reshape(held, frames, width, chans)
    first = spatial[:, 0].reshape(rows, chans).astype(BF16)
    second = spatial[:, 1].reshape(rows, chans).astype(BF16)
    summed = dot(first, time_ref[0]) + dot(second, time_ref[1]) + bias
    feats = (summed / (1.0 + jnp.exp(-summed))).astype(BF16)
    lane = iota((rows, lat_wide), 1)
    lane_h = 2 * (lane // 128) + (lane // 32) % 2
    lane_w = 2 * ((lane // 64) % 2) + (lane // 16) % 2
    keep = (lane_h == h) & (2 * lane_w == iota((rows, lat_wide), 0) % width)
    return jnp.where(keep, dot_nt(feats, latent), 0.0)


def pack_messages(latents, slot_row, ranked, width, out_ref):
    owners = out_ref.shape[0]
    rows = latents.shape[0]
    held = ranked.shape[0]
    latents = latents.astype(BF16)
    shape = (8 * owners, held)
    sub = iota(shape, 0) % 8
    mine = (2 * (iota(shape, 0) // 8) + sub // 2).astype(F32) == slot_row
    hit = one_hot(mine & (sub < 4))
    wide = dot(hit, one_hot(iota((held, rows), 0) == iota((held, rows), 1) // width))
    even = iota((8 * owners, rows), 0) % 2 == 0
    packed = dot(jnp.where(even, wide, 0.0).astype(BF16), latents[:, 0:128])
    packed = packed + dot(jnp.where(even, 0.0, wide).astype(BF16), latents[:, 128:256])
    owner = jnp.floor(slot_row * 0.5)
    hit = ((iota(shape, 0) // 8).astype(F32) == owner) & (sub == 4)
    packed = packed + dot(one_hot(hit), ranked)
    out_ref[...] = packed.astype(BF16).reshape(owners, 8, 128)


def unpack_messages(arrived, block_ref, field_ref):
    loaders = arrived.shape[0]
    slots = 2 * loaders
    flat = arrived.reshape(8 * loaders, 128)
    shape = (slots, 8 * loaders)
    base = 8 * (iota(shape, 0) // 2) + 2 * (iota(shape, 0) % 2)
    block_ref[:, 0:128] = dot(one_hot(iota(shape, 1) == base), flat).astype(BF16)
    block_ref[:, 128:256] = dot(one_hot(iota(shape, 1) == base + 1), flat).astype(BF16)
    both = dot(one_hot(iota(shape, 1) == 8 * (iota(shape, 0) // 2) + 4), flat)
    odd = iota((slots, META), 0) % 2 == 1
    fields = jnp.where(odd, pltpu.roll(both, META - 8, axis=1), both)
    pick = one_hot(iota((8, META), 0) == iota((8, META), 1))
    turned = dot_nt(pick, fields.astype(BF16))
    wide = jnp.concatenate([turned, jnp.zeros((8, META - slots), F32)], axis=1)
    field_ref[...] = wide.astype(BF16)


def sincos(angle):
    turns = jnp.floor(angle * (0.5 / math.pi) + 0.5)
    r = angle - turns * 6.28125
    r = r - turns * (2.0 * math.pi - 6.28125)
    z = r * r
    s = jnp.full_like(z, -1.0 / math.factorial(15))
    for n in (13, 11, 9, 7, 5, 3, 1):
        s = s * z + (1.0 if n % 4 == 1 else -1.0) / math.factorial(n)
    c = jnp.full_like(z, 1.0 / math.factorial(16))
    for n in (14, 12, 10, 8, 6, 4, 2, 0):
        c = c * z + (1.0 if n % 4 == 0 else -1.0) / math.factorial(n)
    return s * r, c


def axis_masks(shape):
    pair = iota(shape, 1) % 64
    return pair < 22, (pair >= 22) & (pair < 43), pair >= 43


def swap_halves(u):
    lane = iota(u.shape, 1)
    turned = pltpu.roll(u, 64, axis=1)
    return jnp.where(lane < 64, -turned, turned)


def rotary_tables(freq):
    shape = (FIELDS, META)
    sub = iota(shape, 0)
    in_f, in_r, in_c = axis_masks(shape)
    step = jnp.where((sub == 1) & in_f, 1.0, 0.0)
    step = jnp.where(((sub == 2) & in_r) | ((sub == 3) & in_c), 2.0, step)
    rest = jnp.broadcast_to(freq, shape)
    tables = []
    for _ in range(3):
        part = rest.astype(BF16).astype(F32)
        rest = rest - part
        tables.append((step * part).astype(BF16))
    return jnp.concatenate(tables + [step.astype(BF16)], axis=1)


def token_weights(ew_ref, freq, first):
    base = ew_ref[:, first : first + 128]
    shape = (8, 128)
    in_f, in_r, in_c = axis_masks(shape)
    blocks = []
    for tok in range(4):
        offset = jnp.where(in_r, float(tok // 2), 0.0) + jnp.where(in_c, float(tok % 2), 0.0)
        s, c = sincos(jnp.broadcast_to(freq, shape) * offset)
        turned = base * c[0:1, :] + swap_halves(base) * s[0:1, :]
        blocks.append(jnp.concatenate([turned, swap_halves(turned)], axis=1))
    return jnp.concatenate(blocks, axis=0)


def from_fields(fields, tables):
    wide = dot_tn(fields, tables)
    angle = wide[:, 0:128] + wide[:, 128:256] + wide[:, 256:384]
    s, c = sincos(angle)
    return s, c, wide[:, 384:512]


def project_keys(batch, block_ref, field_ref, tables, wk, wv, keys_ref, vals_ref):
    blocks, slots, _ = block_ref.shape
    tiles = blocks * slots
    wide = [dot_tn(field_ref[i, :, 0:slots], tables) for i in range(blocks)]
    wide = jnp.concatenate(wide, axis=0)
    s, c = sincos(wide[:, 0:128] + wide[:, 128:256] + wide[:, 256:384])
    pos = wide[:, 384:512]
    pick = one_hot((iota((FIELDS, META), 0) == 4) & (iota((FIELDS, META), 1) == 0))
    live = jnp.concatenate([dot_tn(field_ref[i, :, 0:slots], pick) for i in range(blocks)], axis=0)
    dead = jnp.where(iota((tiles, META), 1) == 0, (live - 1.0) * BIG, 0.0).astype(BF16)
    lat = block_ref[...].reshape(tiles, 256)
    in_f, in_r, in_c = axis_masks((1, 128))
    for tok in range(4):
        at = (batch * 4 + tok) * tiles
        here = iota((256, 1), 0) // 64 == tok
        u = dot(lat, jnp.where(here, wk, 0.0).astype(BF16))
        k = u[:, 0:128] * c + u[:, 128:256] * s
        shift = jnp.where(in_r, float(tok // 2), 0.0) + jnp.where(in_c, float(tok % 2), 0.0)
        keys_ref[at : at + tiles, 0:128] = dead
        keys_ref[at : at + tiles, 128:256] = k.astype(BF16)
        keys_ref[at : at + tiles, 256:384] = (k * (pos + shift)).astype(BF16)
        vals_ref[at : at + tiles, :] = dot(lat, jnp.where(here, wv, 0.0).astype(BF16)).astype(BF16)


def project_queries(lat, fields, tables, wq):
    slots = lat.shape[0]
    tokens = 4 * slots
    taken = (iota((tokens, slots), 0) // 4).astype(F32) == fields[0:1, :].astype(F32)
    chosen = one_hot(taken & (fields[4:5, :].astype(F32) > 0.5))
    which = iota((tokens, 256), 0) % 4 == iota((tokens, 256), 1) // 64
    my_lat = jnp.where(which, dot(chosen, lat), 0.0).astype(BF16)
    my_fields = dot_nt(fields, chosen).astype(BF16)
    s, c, pos = from_fields(my_fields, tables)
    pick = one_hot(iota((FIELDS, META), 0) == 4)
    live = dot_tn(my_fields, pick)
    u = dot(my_lat, wq.astype(BF16))
    q = u[:, 0:128] * c + u[:, 128:256] * s
    in_f, in_r, in_c = axis_masks((tokens, 128))
    tok = iota((tokens, 128), 0) % 4
    pos = pos + jnp.where(in_r & (tok >= 2), 1.0, 0.0) + jnp.where(in_c & (tok % 2 == 1), 1.0, 0.0)
    lane0 = one_hot(iota((tokens, META), 1) == 0)
    scale = 128.0 ** (-0.5) * math.log2(math.e)
    q_ext = jnp.concatenate([lane0, (q * scale).astype(BF16)], axis=1)
    return q, q_ext, pos, live


def finish_attention(q, q_ext, pos, live, top, cot_ref, out_ref, keys_ref, vals_ref, score_ref):
    tokens = q.shape[0]
    keys = keys_ref.shape[0]
    chunk = min(512, keys)
    starts = range(0, keys, chunk)
    top = jnp.max(top, axis=1, keepdims=True)
    sums = jnp.zeros((tokens, chunk), F32)
    mixed = jnp.zeros((tokens, 128), F32)
    for at in starts:
        weights = jnp.exp2(score_ref[:, at : at + chunk] - top)
        score_ref[:, at : at + chunk] = weights
        sums = sums + weights
        mixed = mixed + dot(weights.astype(BF16), vals_ref[at : at + chunk, :])
    inv = 1.0 / jnp.sum(sums, axis=1, keepdims=True)
    mixed = mixed * inv
    out_ref[...] = (mixed * live).astype(BF16)
    cot = cot_ref[...]
    mean = jnp.sum(cot.astype(F32) * mixed, axis=1, keepdims=True)
    back = jnp.zeros((tokens, 256), F32)
    for at in starts:
        dprob = dot_nt(cot, vals_ref[at : at + chunk, :])
        dscore = score_ref[:, at : at + chunk] * (dprob - mean)
        back = back + dot(dscore.astype(BF16), keys_ref[at : at + chunk, 128:384])
    g = pltpu.roll(back[:, 0:128], 64, axis=1)
    gp = pltpu.roll(back[:, 128:256], 64, axis=1)
    terms = q * (pos * g - gp) * (inv * 128.0 ** (-0.5) * live)
    line = jnp.sum(terms, axis=0, keepdims=True)
    other = pltpu.roll(line, 64, axis=1)
    return jnp.where(iota((1, 128), 1) < 64, line - other, other - line)


def greet():
    me_dp, me_seq = lax.axis_index("dp"), lax.axis_index("seq")
    n_dp, n_seq = lax.axis_size("dp"), lax.axis_size("seq")
    barrier = pltpu.get_barrier_semaphore()

    def to_dp(i, _):
        peer = lax.rem(me_dp + i, n_dp)
        pl.semaphore_signal(barrier, inc=1, device_id=(peer, me_seq), device_id_type=MESH)
        return 0

    def to_seq(i, _):
        peer = lax.rem(me_seq + i, n_seq)
        pl.semaphore_signal(barrier, inc=1, device_id=(me_dp, peer), device_id_type=MESH)
        return 0

    lax.fori_loop(1, n_dp, to_dp, 0)
    lax.fori_loop(1, n_seq, to_seq, 0)
    return barrier, n_dp + n_seq - 2


def spread(axis, src_of, dst_ref, send_sem, recv_sem):
    me_dp, me_seq = lax.axis_index("dp"), lax.axis_index("seq")
    n = lax.axis_size(axis)
    me = lax.axis_index(axis)

    def copy(peer, slot):
        where = (peer, me_seq) if axis == "dp" else (me_dp, peer)
        return pltpu.make_async_remote_copy(
            src_ref=src_of(peer),
            dst_ref=dst_ref.at[slot],
            send_sem=send_sem.at[peer],
            recv_sem=recv_sem.at[slot],
            device_id=where,
            device_id_type=MESH,
        )

    def each(act):
        def body(i, _):
            act(lax.rem(me + i, n))
            return 0

        lax.fori_loop(1, n, body, 0)

    def start():
        each(lambda peer: copy(peer, me).start())

    def wait_recv():
        each(lambda peer: copy(peer, peer).wait_recv())

    def wait_send():
        each(lambda peer: copy(peer, me).wait_send())

    return start, wait_recv, wait_send


def fold_load(embed_ref, qkv_ref, unit, window, columns, sems):
    shard = qkv_ref.shape[0]
    wide = window.shape[1]
    first = (lax.axis_index("seq") * shard) // 128 * 128
    rows = pl.ds(pl.multiple_of(8 * (unit // 3), 8), 8)
    cols = pl.ds(pl.multiple_of(128 * (unit % 3), 128), 128)
    left = pltpu.make_async_copy(embed_ref.at[rows, pl.ds(pl.multiple_of(first, 128), wide)], window, sems.at[0])
    right = pltpu.make_async_copy(qkv_ref.at[:, cols], columns, sems.at[1])
    left.start()
    right.start()
    return left, right


def fold_partial(window, columns):
    shard = columns.shape[0]
    wide = window.shape[1]
    part = window[...].astype(F32)
    if wide != shard:
        odd = lax.axis_index("seq") % 2 == 1
        part = jnp.where(odd, pltpu.roll(part, wide - 64, axis=1), part)
    return dot(part[:, 0:shard].astype(BF16), columns[...])


def turn_weights(source, chans, taps, target):
    for slot, tap in enumerate(taps):
        part = source[:, tap * chans : (tap + 1) * chans].astype(F32)
        target[slot] = part.T.astype(BF16)


def whole_kernel(
    tiles_hbm,
    dest_hbm,
    meta_hbm,
    space_hbm,
    time_hbm,
    bias_hbm,
    latent_hbm,
    embed_hbm,
    qkv_hbm,
    freq_hbm,
    cot_hbm,
    out_ref,
    grad_ref,
    tiles,
    dest,
    meta,
    space_raw,
    time_raw,
    bias,
    latent,
    freq_in,
    cot,
    window,
    columns,
    load_sem,
    tile_sem,
    fold_sem,
    space,
    time,
    messages,
    arrived,
    blocks,
    fields,
    parts,
    unit_buf,
    unit_all,
    ew,
    keys_ref,
    vals_ref,
    score_ref,
    line,
    mid,
    by_seq,
    by_dp,
    part_send,
    part_recv,
    unit_send,
    unit_recv,
    msg_send,
    msg_recv,
    ring_send,
    ring_recv,
    seq_send,
    seq_recv,
    dp_send,
    dp_recv,
):
    me_dp, me_seq = lax.axis_index("dp"), lax.axis_index("seq")
    n_dp, n_seq = lax.axis_size("dp"), lax.axis_size("seq")
    held, _, height, width, chans = tiles.shape
    per = parts.shape[1]

    loads = []
    pairs = [(dest_hbm, dest), (meta_hbm, meta), (space_hbm, space_raw), (time_hbm, time_raw), (bias_hbm, bias)]
    pairs += [(latent_hbm, latent), (freq_hbm, freq_in), (cot_hbm, cot)]
    for i, (source, target) in enumerate(pairs):
        loads.append(pltpu.make_async_copy(source, target, load_sem.at[i]))
        loads[-1].start()
    folds = []
    for j in range(per):
        unit = lax.rem(me_dp * per + j, UNITS)
        folds.append(fold_load(embed_hbm, qkv_hbm, unit, window.at[j], columns.at[j], fold_sem.at[j]))
    chunks = []
    for i in range(height // 2):
        rows = pl.ds(2 * i, 2)
        chunks.append(pltpu.make_async_copy(tiles_hbm.at[:, :, rows], tiles.at[:, :, rows], tile_sem.at[i]))
        chunks[-1].start()
    barrier, count = greet()

    for load in loads:
        load.wait()
    for left, right in folds:
        left.wait()
        right.wait()
    for j in range(per):
        parts[me_seq, j] = fold_partial(window.at[j], columns.at[j])
    turn_weights(space_raw, chans, range(9), space)
    turn_weights(time_raw, chans, (1, 2), time)
    slot_row, ranked = place_tiles(dest, meta, n_dp)
    latent_wide = jnp.concatenate([latent[...]] * 16, axis=0)

    start_parts, recv_parts, sent_parts = spread("seq", lambda peer: parts.at[me_seq], parts, part_send, part_recv)
    start_msgs, recv_msgs, sent_msgs = spread("dp", lambda peer: messages.at[peer], arrived, msg_send, msg_recv)
    start_units, recv_units, sent_units = spread("dp", lambda peer: unit_buf, unit_all, unit_send, unit_recv)
    start_seq, recv_seq, sent_seq = spread("seq", lambda peer: line, by_seq, seq_send, seq_recv)
    start_dp, recv_dp, sent_dp = spread("dp", lambda peer: mid, by_dp, dp_send, dp_recv)

    total = None
    for h in range(height // 2):
        if h == 0:
            chunks[0].wait()
        if h + 1 < height // 2:
            chunks[h + 1].wait()
        part = encode_rows(h, tiles, space, time, bias[...], latent_wide)
        total = part if total is None else total + part
        if h == height // 4:
            pl.semaphore_wait(barrier, count)
            start_parts()
    pack_messages(total, slot_row, ranked, width, messages)
    start_msgs()
    arrived[me_dp] = messages[me_dp]
    recv_msgs()
    unpack_messages(arrived[...], blocks.at[0], fields.at[0])

    far = {1: n_seq // 2, -1: (n_seq - 1) // 2}

    def slot_at(way, distance):
        return 2 * distance - 1 if way == 1 else 2 * distance

    def hop(way, source, distance, links):
        to = lax.rem(me_seq + way * links + n_seq, n_seq)
        slot = slot_at(way, distance)
        copies = []
        for kind, buf in enumerate((blocks, fields)):
            copies.append(
                pltpu.make_async_remote_copy(
                    src_ref=buf.at[source],
                    dst_ref=buf.at[slot],
                    send_sem=ring_send.at[kind, slot],
                    recv_sem=ring_recv.at[kind, slot],
                    device_id=(me_dp, to),
                    device_id_type=MESH,
                )
            )
        return copies

    sends = []

    def send(way, source, distance, links):
        for copy in hop(way, source, distance, links):
            copy.start()
            sends.append(copy)

    def receive(distance):
        for way in (1, -1):
            if distance <= far[way]:
                for copy in hop(way, 0, distance, 1):
                    copy.wait_recv()
                if distance + 2 <= far[way]:
                    send(way, slot_at(way, distance), distance + 2, 2)

    for distance in (1, 2):
        for way in (1, -1):
            if distance <= far[way]:
                send(way, 0, distance, distance)

    recv_parts()
    unit_buf[...] = jnp.sum(parts[...], axis=0)
    unit_all[me_dp] = unit_buf[...]
    start_units()

    group = min(4, n_seq)
    slots = blocks.shape[1]
    tokens = 4 * slots
    last = (n_seq // group - 1) * group
    got = 1
    while slot_at(-1, got) < last or slot_at(1, got) < last:
        receive(got)
        got += 1
    recv_units()
    for unit in range(UNITS):
        ew[8 * (unit // 3) : 8 * (unit // 3) + 8, 128 * (unit % 3) : 128 * (unit % 3) + 128] = unit_all[unit // per, unit % per]

    freq = jnp.concatenate([freq_in[...], freq_in[...]], axis=1)
    tables = rotary_tables(freq)
    wq = token_weights(ew, freq, 0)
    wk = token_weights(ew, freq, 128)
    wv = jnp.concatenate([ew[:, 256:384]] * 4, axis=0)
    q, q_ext, pos, live = project_queries(blocks[0], fields[0, :, 0:slots], tables, wq)
    step = group * tokens
    top = jnp.full((tokens, step), -jnp.inf, F32)
    for batch in range(n_seq // group):
        if batch == n_seq // group - 1:
            while got <= far[1]:
                receive(got)
                got += 1
        part = pl.ds(batch * group, group)
        project_keys(batch, blocks.at[part], fields.at[part], tables, wk, wv, keys_ref, vals_ref)
        scores = dot_nt(q_ext, keys_ref[batch * step : (batch + 1) * step, 0:256])
        score_ref[:, batch * step : (batch + 1) * step] = scores
        top = jnp.maximum(top, scores)
    line[...] = finish_attention(q, q_ext, pos, live, top, cot, out_ref, keys_ref, vals_ref, score_ref)

    start_seq()
    by_seq[me_seq] = line[...]
    recv_seq()
    mid[...] = jnp.sum(by_seq[...], axis=0)
    start_dp()
    by_dp[me_dp] = mid[...]
    for copy in sends:
        copy.wait_send()
    sent_msgs()
    sent_parts()
    sent_units()
    sent_seq()
    recv_dp()
    grad_ref[...] = jnp.sum(by_dp[...], axis=0)[:, 0 : grad_ref.shape[1]]
    sent_dp()


def per_device(
    tiles,
    tile_dest,
    tile_meta,
    space_weight,
    time_weight,
    conv_bias,
    latent_weight,
    embed_weight,
    qkv_weight,
    rope_freq,
    cotangent,
):
    n_dp, n_seq = lax.axis_size("dp"), lax.axis_size("seq")
    chans = tiles.shape[-1]
    slots = 2 * n_dp
    tokens = 4 * slots
    keys = tokens * n_seq
    per = -(-UNITS // n_dp)
    shard = qkv_weight.shape[0]
    pairs = rope_freq.shape[0]
    operands = (
        tiles,
        tile_dest[None, :],
        tile_meta.T,
        space_weight.T,
        time_weight.T,
        conv_bias[None, :],
        latent_weight.T,
        embed_weight,
        qkv_weight,
        rope_freq[None, :],
        cotangent,
    )
    dma = pltpu.SemaphoreType.DMA
    buf = pltpu.VMEM
    local = [operands[i] for i in (0, 1, 2, 3, 4, 5, 6, 9, 10)]
    scratch = [buf(a.shape, a.dtype) for a in local]
    scratch += [
        buf((per, 8, -(-shard // 128) * 128), BF16),
        buf((per, shard, 128), BF16),
        dma((8,)),
        dma((tiles.shape[2] // 2,)),
        dma((per, 2)),
        buf((9, chans, chans), BF16),
        buf((2, chans, chans), BF16),
        buf((n_dp, 8, 128), BF16),
        buf((n_dp, 8, 128), BF16),
        buf((n_seq, slots, 256), BF16),
        buf((n_seq, FIELDS, META), BF16),
        buf((n_seq, per, 8, 128), F32),
        buf((per, 8, 128), F32),
        buf((n_dp, per, 8, 128), F32),
        buf((64, 384), F32),
        buf((keys, 384), BF16),
        buf((keys, 128), BF16),
        buf((tokens, keys), F32),
        buf((1, 128), F32),
        buf((1, 128), F32),
        buf((n_seq, 1, 128), F32),
        buf((n_dp, 1, 128), F32),
        dma((n_seq,)),
        dma((n_seq,)),
        dma((n_dp,)),
        dma((n_dp,)),
        dma((n_dp,)),
        dma((n_dp,)),
        dma((2, n_seq)),
        dma((2, n_seq)),
        dma((n_seq,)),
        dma((n_seq,)),
        dma((n_dp,)),
        dma((n_dp,)),
    ]
    vmem = pl.BlockSpec(memory_space=pltpu.VMEM)
    attended, grad = pl.pallas_call(
        whole_kernel,
        out_shape=(
            jax.ShapeDtypeStruct((tokens, 128), BF16),
            jax.ShapeDtypeStruct((1, pairs), F32),
        ),
        in_specs=[pl.BlockSpec(memory_space=pltpu.HBM)] * len(operands),
        out_specs=(vmem, vmem),
        scratch_shapes=scratch,
        compiler_params=pltpu.CompilerParams(
            vmem_limit_bytes=56 << 20, collective_id=0, has_side_effects=True
        ),
    )(*operands)
    return attended, grad[0]


def solution(mesh):
    both = ("dp", "seq")
    specs = (
        P(both, None, None, None, None),
        P(both),
        P(both, None),
        P(),
        P(),
        P(),
        P(),
        P(),
        P("seq", None),
        P(),
        P(both, None),
    )
    return jax.shard_map(
        per_device,
        mesh=mesh,
        in_specs=specs,
        out_specs=(P(both, None), P()),
        check_vma=False,
    )
```

time: 95.9 us -> 64.8 us (0.68)
  Pallas kernels: 87.7 us -> 61.4 us
  other arithmetic: 2.33 us -> 0 us
  local copies, waits for them, and re-layouts: 4.83 us -> 2.59 us
    pallas_call x4 -> x1, Pallas kernels: 87.7 us -> 61.4 us  [per_device(): pl.pallas_call(whole_kernel, out_shape=(jax.ShapeDtypeStruct((tokens, 128...]
    another operation x7 -> x0, local copies, waits for them, and re-layouts: 1.72 us -> none  [the longest x2 0.83 us: per_device(): jnp.tile(latent_weight, (1, 16))]
    unnamed x12 -> x2, local copies, waits for them, and re-layouts: 2.53 us -> 2.59 us
where the time goes in v2:
time: 64.8 us; the launch traced here: 64.6 us
  Pallas kernels  61.4 us (95%)
  local copies, waits for them, and re-layouts  2.59 us (4%)
    pallas_call x1, Pallas kernels, per_device(): pl.pallas_call(whole_kernel, out_shape=(jax.ShapeDtypeStruct((tokens, 128...  61.4 us
    unnamed x2, local copies, waits for them, and re-layouts  2.59 us

profile of v2, /device:TPU:1, one launch (start us, length us, event | category | flops | bytes accessed | tf_op | source)
XLA Modules:
  0.0 64.6 jit_solution(2191981049321353718)
XLA Ops:
  0.6 61.4 %shard_map.122 = (bf16[256,128]{1,0:T(8,128)(2,1)}, f32[1,64]{1,0:T(1,128)}) custom-call(bf16[32,2,8,8,192]{4,3,2,1,0:T(8,128)(2,1)} %tiles_hbm.1, s32[1,32]{1,0:T(1,128)} %bitcast.13, s32[4,32]{1,0:T(4,128)} %bitcast.11, bf16[192,1728]{1,0:T(8,128)(2,1)} %bitcast.8, bf16[192,576]{1,0:T(8,128)(2,1)} %bitcast.9, f32[1,192]{1,0:T(1,128)} %bitcast.12, ...), custom_call_target="tpu_custom_call" | custom-call | tf_op jit(solution)/shard_map/pallas_call | solution.py:631
  62.0 1.5 %copy.15 = bf16[256,128]{1,0:T(8,128)(2,1)} copy(bf16[256,128]{1,0:T(8,128)(2,1)} %get-tuple-element.8) | data formatting | bytes 131072
  63.5 1.1 %copy.16 = f32[64]{0:T(128)} copy(f32[64]{0:T(128)} %bitcast.15) | data formatting | bytes 512

commit v3 on v2

--- a/solution.py
+++ b/solution.py
@@ -14,6 +14,7 @@
 BIG = 1e30
 UNITS = 24
 FIELDS = 8
+STRIDE = 2
 
 
 def iota(shape, dim):
@@ -59,16 +60,13 @@
     held, frames, height, width, chans = tiles_ref.shape
     rows = held * width
     lat_wide = latent.shape[0]
-    shifted = [None, None, None]
-    for row_off in range(3):
-        src = 2 * h + row_off
-        if src >= height:
-            continue
-        x = tiles_ref[:, :, src].reshape(held * frames * width, chans)
-        for col_off in range(3):
-            part = dot(x, space_ref[row_off * 3 + col_off])
-            old = shifted[col_off]
-            shifted[col_off] = part if old is None else old + part
+    deep = space_ref.shape[1] // 3
+    pad = jnp.zeros((held * frames * width, deep - chans), BF16)
+    taps = []
+    for src in range(2 * h, min(2 * h + 3, height)):
+        taps += [tiles_ref[:, :, src].reshape(held * frames * width, chans), pad]
+    x = jnp.concatenate(taps, axis=1)
+    shifted = [dot(x, space_ref[col_off, 0 : x.shape[1], :]) for col_off in range(3)]
     y0, y1, y2 = [y.reshape(held * frames, width, chans) for y in shifted]
     y1 = pltpu.roll(y1, width - 1, axis=1)
     edge = iota((1, width, chans), 1) < width - 2
@@ -85,22 +83,23 @@
     return jnp.where(keep, dot_nt(feats, latent), 0.0)
 
 
-def pack_messages(latents, slot_row, ranked, width, out_ref):
-    owners = out_ref.shape[0]
-    rows = latents.shape[0]
-    held = ranked.shape[0]
-    latents = latents.astype(BF16)
+def packing(slot_row, rows, width, owners):
+    held = slot_row.shape[1]
     shape = (8 * owners, held)
     sub = iota(shape, 0) % 8
     mine = (2 * (iota(shape, 0) // 8) + sub // 2).astype(F32) == slot_row
     hit = one_hot(mine & (sub < 4))
     wide = dot(hit, one_hot(iota((held, rows), 0) == iota((held, rows), 1) // width))
     even = iota((8 * owners, rows), 0) % 2 == 0
-    packed = dot(jnp.where(even, wide, 0.0).astype(BF16), latents[:, 0:128])
-    packed = packed + dot(jnp.where(even, 0.0, wide).astype(BF16), latents[:, 128:256])
     owner = jnp.floor(slot_row * 0.5)
-    hit = ((iota(shape, 0) // 8).astype(F32) == owner) & (sub == 4)
-    packed = packed + dot(one_hot(hit), ranked)
+    named = one_hot(((iota(shape, 0) // 8).astype(F32) == owner) & (sub == 4))
+    return jnp.where(even, wide, 0.0).astype(BF16), jnp.where(even, 0.0, wide).astype(BF16), named
+
+
+def pack_messages(latents, picks, ranked, out_ref):
+    owners = out_ref.shape[0]
+    latents = latents.astype(BF16)
+    packed = dot(picks[0], latents[:, 0:128]) + dot(picks[1], latents[:, 128:256]) + dot(picks[2], ranked)
     out_ref[...] = packed.astype(BF16).reshape(owners, 8, 128)
 
 
@@ -242,7 +241,7 @@
         mixed = mixed + dot(weights.astype(BF16), vals_ref[at : at + chunk, :])
     inv = 1.0 / jnp.sum(sums, axis=1, keepdims=True)
     mixed = mixed * inv
-    out_ref[...] = (mixed * live).astype(BF16)
+    out_ref[...] = mixed * live
     cot = cot_ref[...]
     mean = jnp.sum(cot.astype(F32) * mixed, axis=1, keepdims=True)
     back = jnp.zeros((tokens, 256), F32)
@@ -283,32 +282,28 @@
     n = lax.axis_size(axis)
     me = lax.axis_index(axis)
 
-    def copy(peer, slot):
-        where = (peer, me_seq) if axis == "dp" else (me_dp, peer)
+    def copy(peer, source, target):
         return pltpu.make_async_remote_copy(
-            src_ref=src_of(peer),
-            dst_ref=dst_ref.at[slot],
-            send_sem=send_sem.at[peer],
-            recv_sem=recv_sem.at[slot],
-            device_id=where,
+            src_ref=source,
+            dst_ref=target,
+            send_sem=send_sem,
+            recv_sem=recv_sem,
+            device_id=(peer, me_seq) if axis == "dp" else (me_dp, peer),
             device_id_type=MESH,
         )
 
-    def each(act):
-        def body(i, _):
-            act(lax.rem(me + i, n))
-            return 0
-
-        lax.fori_loop(1, n, body, 0)
-
     def start():
-        each(lambda peer: copy(peer, me).start())
+        for i in range(1, n):
+            peer = lax.rem(me + i, n)
+            copy(peer, src_of(peer), dst_ref.at[me]).start()
+
+    others = dst_ref.at[pl.ds(0, n - 1)]
 
     def wait_recv():
-        each(lambda peer: copy(peer, peer).wait_recv())
+        copy(lax.rem(me + 1, n), others, others).wait_recv()
 
     def wait_send():
-        each(lambda peer: copy(peer, me).wait_send())
+        copy(lax.rem(me + 1, n), others, others).wait_send()
 
     return start, wait_recv, wait_send
 
@@ -336,10 +331,12 @@
     return dot(part[:, 0:shard].astype(BF16), columns[...])
 
 
-def turn_weights(source, chans, taps, target):
-    for slot, tap in enumerate(taps):
-        part = source[:, tap * chans : (tap + 1) * chans].astype(F32)
-        target[slot] = part.T.astype(BF16)
+def turn_weights(source, chans, tap, target):
+    part = source[:, tap * chans : (tap + 1) * chans].astype(F32)
+    target[0:chans, :] = part.T.astype(BF16)
+    rest = target.shape[0] - chans
+    if rest:
+        target[chans:, :] = jnp.zeros((rest, chans), BF16)
 
 
 def whole_kernel(
@@ -424,14 +421,13 @@
 
     for load in loads:
         load.wait()
-    for left, right in folds:
-        left.wait()
-        right.wait()
-    for j in range(per):
-        parts[me_seq, j] = fold_partial(window.at[j], columns.at[j])
-    turn_weights(space_raw, chans, range(9), space)
-    turn_weights(time_raw, chans, (1, 2), time)
     slot_row, ranked = place_tiles(dest, meta, n_dp)
+    picks = packing(slot_row, held * width, width, n_dp)
+    deep = space.shape[1] // 3
+    for tap in range(9):
+        turn_weights(space_raw, chans, tap, space.at[tap % 3, pl.ds(deep * (tap // 3), deep)])
+    for tap in (1, 2):
+        turn_weights(time_raw, chans, tap, time.at[tap - 1])
     latent_wide = jnp.concatenate([latent[...]] * 16, axis=0)
 
     start_parts, recv_parts, sent_parts = spread("seq", lambda peer: parts.at[me_seq], parts, part_send, part_recv)
@@ -448,11 +444,15 @@
             chunks[h + 1].wait()
         part = encode_rows(h, tiles, space, time, bias[...], latent_wide)
         total = part if total is None else total + part
-        if h == height // 4:
-            pl.semaphore_wait(barrier, count)
-            start_parts()
-    pack_messages(total, slot_row, ranked, width, messages)
+    pack_messages(total, picks, ranked, messages)
+    pl.semaphore_wait(barrier, count)
     start_msgs()
+    for left, right in folds:
+        left.wait()
+        right.wait()
+    for j in range(per):
+        parts[me_seq, j] = fold_partial(window.at[j], columns.at[j])
+    start_parts()
     arrived[me_dp] = messages[me_dp]
     recv_msgs()
     unpack_messages(arrived[...], blocks.at[0], fields.at[0])
@@ -491,10 +491,10 @@
             if distance <= far[way]:
                 for copy in hop(way, 0, distance, 1):
                     copy.wait_recv()
-                if distance + 2 <= far[way]:
-                    send(way, slot_at(way, distance), distance + 2, 2)
-
-    for distance in (1, 2):
+                if distance + STRIDE <= far[way]:
+                    send(way, slot_at(way, distance), distance + STRIDE, STRIDE)
+
+    for distance in range(1, STRIDE + 1):
         for way in (1, -1):
             if distance <= far[way]:
                 send(way, 0, distance, distance)
@@ -597,7 +597,7 @@
         dma((8,)),
         dma((tiles.shape[2] // 2,)),
         dma((per, 2)),
-        buf((9, chans, chans), BF16),
+        buf((3, 3 * 256, chans), BF16),
         buf((2, chans, chans), BF16),
         buf((n_dp, 8, 128), BF16),
         buf((n_dp, 8, 128), BF16),
@@ -614,34 +614,34 @@
         buf((1, 128), F32),
         buf((n_seq, 1, 128), F32),
         buf((n_dp, 1, 128), F32),
-        dma((n_seq,)),
-        dma((n_seq,)),
-        dma((n_dp,)),
-        dma((n_dp,)),
-        dma((n_dp,)),
-        dma((n_dp,)),
+        dma(()),
+        dma(()),
+        dma(()),
+        dma(()),
+        dma(()),
+        dma(()),
         dma((2, n_seq)),
         dma((2, n_seq)),
-        dma((n_seq,)),
-        dma((n_seq,)),
-        dma((n_dp,)),
-        dma((n_dp,)),
+        dma(()),
+        dma(()),
+        dma(()),
+        dma(()),
     ]
     vmem = pl.BlockSpec(memory_space=pltpu.VMEM)
     attended, grad = pl.pallas_call(
         whole_kernel,
         out_shape=(
-            jax.ShapeDtypeStruct((tokens, 128), BF16),
+            jax.ShapeDtypeStruct((tokens, 128), F32),
             jax.ShapeDtypeStruct((1, pairs), F32),
         ),
         in_specs=[pl.BlockSpec(memory_space=pltpu.HBM)] * len(operands),
         out_specs=(vmem, vmem),
         scratch_shapes=scratch,
         compiler_params=pltpu.CompilerParams(
-            vmem_limit_bytes=56 << 20, collective_id=0, has_side_effects=True
+            vmem_limit_bytes=24 << 20, collective_id=0, has_side_effects=True
         ),
-    )(*operands)
-    return attended, grad[0]
+    )(*[pltpu.with_memory_space_constraint(a, pltpu.HBM) for a in operands])
+    return attended.astype(BF16), grad[0]
 
 
 def solution(mesh):

time: 64.8 us -> 60.4 us (0.932)
  Pallas kernels: 61.4 us -> 58.5 us
  local copies, waits for them, and re-layouts: 2.59 us -> 0.51 us
    pallas_call x1, Pallas kernels: 61.4 us -> 58.5 us  [per_device(): pl.pallas_call(whole_kernel, out_shape=(jax.ShapeDtypeStruct((tokens, 128...]
    unnamed x2 -> x1, local copies, waits for them, and re-layouts: 2.59 us -> 0.51 us
where the time goes in v3:
time: 60.4 us; the launch traced here: 60.3 us
  Pallas kernels  58.5 us (97%)
  other arithmetic  0.64 us (1%)
  between operations  0.64 us (1%)
    pallas_call x1, Pallas kernels, per_device(): pl.pallas_call(whole_kernel, out_shape=(jax.ShapeDtypeStruct((tokens, 128...  58.5 us

profile of v3, /device:TPU:1, one launch (start us, length us, event | category | flops | bytes accessed | tf_op | source)
XLA Modules:
  0.0 60.3 jit_solution(12132724418946007992)
XLA Ops:
  0.6 58.5 %shard_map.122 = (f32[256,128]{1,0:T(8,128)S(1)}, f32[1,64]{1,0:T(1,128)S(1)}) custom-call(bf16[32,2,8,8,192]{4,3,2,1,0:T(8,128)(2,1)} %tiles_hbm.1, s32[1,32]{1,0:T(1,128)} %bitcast.14, s32[4,32]{1,0:T(4,128)} %bitcast.12, bf16[192,1728]{1,0:T(8,128)(2,1)} %bitcast.9, bf16[192,576]{1,0:T(8,128)(2,1)} %bitcast.10, f32[1,192]{1,0:T(1,128)} %bitcast.13, ...), custom_call_target="tpu_custom_call" | custom-call | tf_op jit(solution)/shard_map/pallas_call | solution.py:631
  59.1 0.6 %convert_element_type.3 = bf16[256,128]{1,0:T(8,128)(2,1)} convert(f32[256,128]{1,0:T(8,128)S(1)} %get-tuple-element.4) | non-fusion elementwise | flops 32768 | bytes 196608 | tf_op jit(solution)/shard_map/convert_element_type | solution.py:644
  59.7 0.5 copy.14

commit v4 on v3

--- a/solution.py
+++ b/solution.py
@@ -257,24 +257,15 @@
     return jnp.where(iota((1, 128), 1) < 64, line - other, other - line)
 
 
-def greet():
+def greet(axis):
     me_dp, me_seq = lax.axis_index("dp"), lax.axis_index("seq")
-    n_dp, n_seq = lax.axis_size("dp"), lax.axis_size("seq")
+    n, me = lax.axis_size(axis), lax.axis_index(axis)
     barrier = pltpu.get_barrier_semaphore()
-
-    def to_dp(i, _):
-        peer = lax.rem(me_dp + i, n_dp)
-        pl.semaphore_signal(barrier, inc=1, device_id=(peer, me_seq), device_id_type=MESH)
-        return 0
-
-    def to_seq(i, _):
-        peer = lax.rem(me_seq + i, n_seq)
-        pl.semaphore_signal(barrier, inc=1, device_id=(me_dp, peer), device_id_type=MESH)
-        return 0
-
-    lax.fori_loop(1, n_dp, to_dp, 0)
-    lax.fori_loop(1, n_seq, to_seq, 0)
-    return barrier, n_dp + n_seq - 2
+    for i in sorted(range(1, n), key=lambda i: -min(i, n - i)):
+        peer = lax.rem(me + i, n)
+        where = (peer, me_seq) if axis == "dp" else (me_dp, peer)
+        pl.semaphore_signal(barrier, inc=1, device_id=where, device_id_type=MESH)
+    return n - 1
 
 
 def spread(axis, src_of, dst_ref, send_sem, recv_sem):
@@ -402,6 +393,7 @@
     held, _, height, width, chans = tiles.shape
     per = parts.shape[1]
 
+    count = greet("seq")
     loads = []
     pairs = [(dest_hbm, dest), (meta_hbm, meta), (space_hbm, space_raw), (time_hbm, time_raw), (bias_hbm, bias)]
     pairs += [(latent_hbm, latent), (freq_hbm, freq_in), (cot_hbm, cot)]
@@ -417,7 +409,7 @@
         rows = pl.ds(2 * i, 2)
         chunks.append(pltpu.make_async_copy(tiles_hbm.at[:, :, rows], tiles.at[:, :, rows], tile_sem.at[i]))
         chunks[-1].start()
-    barrier, count = greet()
+    count += greet("dp")
 
     for load in loads:
         load.wait()
@@ -445,7 +437,7 @@
         part = encode_rows(h, tiles, space, time, bias[...], latent_wide)
         total = part if total is None else total + part
     pack_messages(total, picks, ranked, messages)
-    pl.semaphore_wait(barrier, count)
+    pl.semaphore_wait(pltpu.get_barrier_semaphore(), count)
     start_msgs()
     for left, right in folds:
         left.wait()

time: 60.4 us -> 59.5 us (0.985)
  Pallas kernels: 58.5 us -> 57.6 us
    pallas_call x1, Pallas kernels: 58.5 us -> 57.6 us  [per_device(): pl.pallas_call(whole_kernel, out_shape=(jax.ShapeDtypeStruct((tokens, 128...]
where the time goes in v4:
time: 59.5 us; the launch traced here: 59.4 us
  Pallas kernels  57.6 us (97%)
  other arithmetic  0.64 us (1%)
  between operations  0.64 us (1%)
    pallas_call x1, Pallas kernels, per_device(): pl.pallas_call(whole_kernel, out_shape=(jax.ShapeDtypeStruct((tokens, 128...  57.6 us

profile of v4, /device:TPU:1, one launch (start us, length us, event | category | flops | bytes accessed | tf_op | source)
XLA Modules:
  0.0 59.4 jit_solution(305895671508033475)
XLA Ops:
  0.6 57.6 %shard_map.122 = (f32[256,128]{1,0:T(8,128)S(1)}, f32[1,64]{1,0:T(1,128)S(1)}) custom-call(bf16[32,2,8,8,192]{4,3,2,1,0:T(8,128)(2,1)} %tiles_hbm.1, s32[1,32]{1,0:T(1,128)} %bitcast.14, s32[4,32]{1,0:T(4,128)} %bitcast.12, bf16[192,1728]{1,0:T(8,128)(2,1)} %bitcast.9, bf16[192,576]{1,0:T(8,128)(2,1)} %bitcast.10, f32[1,192]{1,0:T(1,128)} %bitcast.13, ...), custom_call_target="tpu_custom_call" | custom-call | tf_op jit(solution)/shard_map/pallas_call | solution.py:623
  58.2 0.6 %convert_element_type.3 = bf16[256,128]{1,0:T(8,128)(2,1)} convert(f32[256,128]{1,0:T(8,128)S(1)} %get-tuple-element.4) | non-fusion elementwise | flops 32768 | bytes 196608 | tf_op jit(solution)/shard_map/convert_element_type | solution.py:636
  58.9 0.5 copy.14

commit v5 on v4

--- a/solution.py
+++ b/solution.py
@@ -411,10 +411,12 @@
         chunks[-1].start()
     count += greet("dp")
 
-    for load in loads:
+    for load in loads[0:2]:
         load.wait()
     slot_row, ranked = place_tiles(dest, meta, n_dp)
     picks = packing(slot_row, held * width, width, n_dp)
+    for load in loads[2:]:
+        load.wait()
     deep = space.shape[1] // 3
     for tap in range(9):
         turn_weights(space_raw, chans, tap, space.at[tap % 3, pl.ds(deep * (tap // 3), deep)])

time: 59.5 us -> 59.3 us (level)
  no operation moved by 1% of the time
where the time goes in v5:
time: 59.3 us; the launch traced here: 59.1 us
  Pallas kernels  57.3 us (97%)
  other arithmetic  0.64 us (1%)
  between operations  0.64 us (1%)
    pallas_call x1, Pallas kernels, per_device(): pl.pallas_call(whole_kernel, out_shape=(jax.ShapeDtypeStruct((tokens, 128...  57.3 us

profile of v5, /device:TPU:1, one launch (start us, length us, event | category | flops | bytes accessed | tf_op | source)
XLA Modules:
  0.0 59.1 jit_solution(14833319330651796612)
XLA Ops:
  0.6 57.3 %shard_map.122 = (f32[256,128]{1,0:T(8,128)S(1)}, f32[1,64]{1,0:T(1,128)S(1)}) custom-call(bf16[32,2,8,8,192]{4,3,2,1,0:T(8,128)(2,1)} %tiles_hbm.1, s32[1,32]{1,0:T(1,128)} %bitcast.14, s32[4,32]{1,0:T(4,128)} %bitcast.12, bf16[192,1728]{1,0:T(8,128)(2,1)} %bitcast.9, bf16[192,576]{1,0:T(8,128)(2,1)} %bitcast.10, f32[1,192]{1,0:T(1,128)} %bitcast.13, ...), custom_call_target="tpu_custom_call" | custom-call | tf_op jit(solution)/shard_map/pallas_call | solution.py:625
  58.0 0.6 %convert_element_type.3 = bf16[256,128]{1,0:T(8,128)(2,1)} convert(f32[256,128]{1,0:T(8,128)S(1)} %get-tuple-element.4) | non-fusion elementwise | flops 32768 | bytes 196608 | tf_op jit(solution)/shard_map/convert_element_type | solution.py:638
  58.6 0.5 copy.14
